TPU v7x, 32 devices: a whole 2x2x4 slice. The times are simulated.
32 devices in a mesh: gx: 8 (over y, x, core), gy: 4 (over z).
Axes of the slice: x: 2, y: 2, z: 4, core: 2. Of those that a mesh axis runs over, the one named last changes fastest.
Arguments:
- fractions: float32 [8, 4, 3, 1024], P('gx', 'gy'), may hold values from 0 to 1
- velocity: float32 [8, 4, 3, 1024], P('gx', 'gy'), may hold values from -4 to 4
- drag_rate: float32 [8, 4, 1024], P('gx', 'gy'), may hold values from 0.5 to 4
- volume: float32 [8, 4, 1024], P('gx', 'gy'), may hold values from 0.25 to 1
- owner: int32 [8, 4, 1024, 1], P('gx', 'gy'), may hold values from 0 to 31, as said below
- element: int32 [8, 4, 1024], P('gx', 'gy'), may hold values from 0 to 31
- coords: int32 [8, 4, 3, 1024], P('gx', 'gy'), may hold values from 0 to 63
- fluid: bfloat16 [8, 4, 32, 6, 512], P('gx', 'gy'), may hold values from -4 to 4
Outputs:
- particle_force: float32 [8, 4, 3, 1024], P('gx', 'gy')
- bin_field: float32 [4, 128, 64, 512], P(None, 'gx', 'gy')
Inputs may be any that keep to these rules, and one draw needn't show every extreme that they name: owner names a device as its gx index times the number of gy indices plus its gy index: the particle's own device or one whose gx and gy indices each differ from it by at most one (no wrap). A particle owned by a device with gx index one lower has first fraction below 0.2, one higher at least 0.8, the same gx index from 0.2 to 0.8; likewise for gy and the second fraction. Among one device's 1024 particles at most 64 have any one other device as owner, and in every device exactly 64 have one of them.
All inputs are finite; a program needn't handle non-finite values.
Results may differ from a plain program's by a relative error of at most 0.00099.
Values may be sent and summed in bfloat16 or wider, within the bound.
No kernel may reach another device: no remote copies, remote signals or barrier semaphores. Data moves between devices by JAX's collectives and lax.ppermute only.
A program may use at most 64 MiB of HBM per device.

v0:
```python
import jax
import jax.numpy as jnp
import numpy as np
from jax import lax
from jax.sharding import PartitionSpec as P

P_DEV = 1024
E_DEV = 32
BINS_THIRD_AXIS = 512
BX = 16
BY = 16
MARGIN = 4
QUANT = 64
CAP = 64


GLL_NODES = (
    -1.0,
    -0.8717401485096066,
    -0.5917001814331423,
    -0.2092992179024789,
    0.2092992179024789,
    0.5917001814331423,
    0.8717401485096066,
    1.0,
)
STIFFNESS = 0.5
PAIR_WIDTH = 0.3
FILTER_BINS = 3.0


def padded(block, sides, width):
    for axis, dim in sides:
        count = lax.axis_size(axis)
        forward = [(i, i + 1) for i in range(count - 1)]
        backward = [(target, source) for source, target in forward]
        low = lax.ppermute(
            lax.slice_in_dim(block, block.shape[dim] - width, None, axis=dim), axis, forward
        )
        high = lax.ppermute(lax.slice_in_dim(block, 0, width, axis=dim), axis, backward)
        block = jnp.concatenate([low, block, high], axis=dim)
    return block


def basis_table(levels):
    points = -1.0 + (2.0 * np.arange(levels) + 1.0) / levels
    lagrange = np.ones((levels, 8))
    for node_a in range(8):
        for node_b in range(8):
            if node_b != node_a:
                lagrange[:, node_a] *= (points - GLL_NODES[node_b]) / (
                    GLL_NODES[node_a] - GLL_NODES[node_b]
                )
    return jnp.asarray(lagrange, dtype=jnp.float32)


def place(fractions, slab_x, slab_y):
    return jnp.stack(
        [slab_x + fractions[0], slab_y + fractions[1], fractions[2] * (BINS_THIRD_AXIS / BX)]
    )


def gaussian_rows(along, centres, deviation):
    distance = along[:, None] - centres[None, :]
    bumps = jnp.exp(-(distance * distance) / (2.0 * deviation * deviation))
    return bumps / jnp.sum(bumps, axis=1, keepdims=True)


def window_cube(positions, loads, slab_x, slab_y, span_x, span_y):
    first_extent = BX + 2 * MARGIN
    second_extent = BY + 2 * MARGIN
    centre_x = slab_x + (jnp.arange(first_extent, dtype=jnp.float32) - MARGIN + 0.5) / BX
    centre_y = slab_y + (jnp.arange(second_extent, dtype=jnp.float32) - MARGIN + 0.5) / BY
    centre_z = (jnp.arange(BINS_THIRD_AXIS, dtype=jnp.float32) + 0.5) / BX
    along_x = gaussian_rows(positions[0], centre_x, FILTER_BINS / BX)[
        :, span_x[0] : span_x[0] + span_x[1]
    ]
    along_y = gaussian_rows(positions[1], centre_y, FILTER_BINS / BY)[
        :, span_y[0] : span_y[0] + span_y[1]
    ]
    along_depth = gaussian_rows(positions[2], centre_z, FILTER_BINS / BX).astype(jnp.bfloat16)
    plane = (along_x[:, :, None] * along_y[:, None, :]).reshape(
        positions.shape[1], span_x[1] * span_y[1]
    )
    scattered_loads = (loads[:, :, None] * plane[None, :, :]).astype(jnp.bfloat16)
    filter_cube = jnp.einsum(
        "vtn,tl->vnl", scattered_loads, along_depth, preferred_element_type=jnp.float32
    )
    return filter_cube.reshape(4, span_x[1], span_y[1], BINS_THIRD_AXIS)


def pair_forces(own, blocks, present):
    particles = own.shape[1]
    row_count = min(512, particles)
    groups = particles // row_count
    stacked = own.reshape(3, groups, row_count).transpose(1, 0, 2)

    def one_group(subset):
        summed = jnp.zeros((3, row_count), own.dtype)
        for ghost_block, weight in zip(blocks, present):
            offset = subset[:, :, None] - ghost_block[:, None, :]
            closeness = (
                jnp.exp(-jnp.sum(offset * offset, axis=0) / (2.0 * PAIR_WIDTH * PAIR_WIDTH))
                * weight
            )
            summed = summed + jnp.sum(offset * closeness[None, :, :], axis=2)
        return summed

    return STIFFNESS * lax.map(one_group, stacked).transpose(1, 0, 2).reshape(3, particles)


def interpolate_slots(flat, fluid, lagrange):
    slots = flat.shape[1]
    levels = jnp.arange(QUANT, dtype=jnp.int32)
    factors = []
    for column in range(3):
        select = (flat[1 + column][None, :] == levels[:, None]).astype(jnp.float32)
        factors.append(
            jnp.dot(
                lagrange.T,
                select,
                precision=lax.Precision.HIGHEST,
                preferred_element_type=jnp.float32,
            )
        )
    weights = (
        (factors[0][:, None, None, :] * factors[1][None, :, None, :] * factors[2][None, None, :, :])
        .reshape(512, slots)
        .astype(jnp.bfloat16)
    )
    table = fluid.reshape(E_DEV * 6, 512)
    projected = jnp.dot(table, weights, preferred_element_type=jnp.float32).reshape(E_DEV, 6, slots)
    picked = (flat[0][None, :] == jnp.arange(E_DEV, dtype=jnp.int32)[:, None]).astype(jnp.float32)
    values = jnp.sum(projected * picked[:, None, :], axis=0)
    return values.astype(jnp.bfloat16)


def flatten_blocks(blocks):
    return blocks.transpose(2, 0, 1, 3).reshape(blocks.shape[2], 9 * CAP)


def unflatten_blocks(values):
    return values.reshape(values.shape[0], 3, 3, CAP).transpose(1, 2, 0, 3)


def margin_spans(inner):
    return ((-1, inner + MARGIN, 0, MARGIN), (0, MARGIN, 0, inner), (1, 0, inner - MARGIN, MARGIN))


def body(fractions, velocity, drag_rate, volume, owner, element, coords, fluid):
    grid_x = lax.axis_size("gx")
    grid_y = lax.axis_size("gy")
    index_x = lax.axis_index("gx")
    index_y = lax.axis_index("gy")
    slab_x = index_x.astype(jnp.float32)
    slab_y = index_y.astype(jnp.float32)
    lagrange = basis_table(QUANT)
    targets = owner.reshape(P_DEV)
    step_x = targets // grid_y - index_x
    step_y = targets % grid_y - index_y
    code = (step_x + 1) * 3 + step_y + 1
    remote = code != 4
    chosen = (code[:, None] == jnp.arange(9, dtype=jnp.int32)[None, :]).astype(jnp.bfloat16)
    order = jnp.arange(P_DEV, dtype=jnp.int32)
    earlier = (order[None, :] < order[:, None]).astype(jnp.bfloat16)
    ranks = jnp.dot(earlier, chosen, preferred_element_type=jnp.float32)
    slot = jnp.sum(ranks * chosen.astype(jnp.float32), axis=1).astype(jnp.int32)
    position_index = jnp.where(remote, code * CAP + slot, 9 * CAP)
    payload = jnp.concatenate([element.reshape(1, P_DEV), coords.reshape(3, P_DEV)], axis=0)
    outgoing = (
        jnp.zeros((4, 9 * CAP + 1), jnp.int32).at[:, position_index].set(payload)[:, : 9 * CAP]
    )
    outgoing = outgoing.reshape(4, 3, 3, CAP).transpose(1, 2, 0, 3)
    own_values = interpolate_slots(payload, fluid, lagrange)
    arrived = padded(outgoing, (("gx", 0), ("gy", 1)), 1)[::2, ::2]
    served = unflatten_blocks(interpolate_slots(flatten_blocks(arrived), fluid, lagrange))
    returned = padded(served, (("gx", 0), ("gy", 1)), 1)[::2, ::2]
    remote_values = flatten_blocks(returned)[:, jnp.minimum(position_index, 9 * CAP - 1)]
    fetched = jnp.where(remote[None, :], remote_values, own_values).astype(jnp.float32)
    ghosts = padded(fractions, (("gx", 0), ("gy", 1)), 1)
    blocks = []
    present = []
    for shift_x in (-1, 0, 1):
        for shift_y in (-1, 0, 1):
            blocks.append(
                place(ghosts[1 + shift_x, 1 + shift_y], slab_x + shift_x, slab_y + shift_y)
            )
            inside = (
                (index_x + shift_x >= 0)
                & (index_x + shift_x < grid_x)
                & (index_y + shift_y >= 0)
                & (index_y + shift_y < grid_y)
            )
            present.append(inside.astype(jnp.float32))
    own = place(fractions[0, 0], slab_x, slab_y)
    pair = pair_forces(own, blocks, present)
    force = (
        drag_rate.reshape(1, P_DEV) * (fetched[0:3] - velocity[0, 0])
        - volume.reshape(1, P_DEV) * fetched[3:6]
        + pair
    )
    loads = jnp.concatenate([force, volume.reshape(1, P_DEV)], axis=0)
    field = jnp.zeros((4, BX, BY, BINS_THIRD_AXIS), jnp.float32)
    ghost_loads = padded(loads.reshape(1, 1, 4, P_DEV), (("gx", 0), ("gy", 1)), 1)
    for shift_x, source_x, target_x, length_x in margin_spans(BX):
        for shift_y, source_y, target_y, length_y in margin_spans(BY):
            piece = window_cube(
                blocks[3 * (shift_x + 1) + shift_y + 1],
                ghost_loads[1 + shift_x, 1 + shift_y],
                slab_x + shift_x,
                slab_y + shift_y,
                (source_x, length_x),
                (source_y, length_y),
            )
            field = field.at[:, target_x : target_x + length_x, target_y : target_y + length_y].add(
                piece
            )
    bin_field = field * (BX * BY * BINS_THIRD_AXIS / P_DEV)
    return (force.reshape(1, 1, 3, P_DEV), bin_field)


def solution(mesh):
    return jax.shard_map(
        body,
        mesh=mesh,
        in_specs=(
            P("gx", "gy", None, None),
            P("gx", "gy", None, None),
            P("gx", "gy", None),
            P("gx", "gy", None),
            P("gx", "gy", None, None),
            P("gx", "gy", None),
            P("gx", "gy", None, None),
            P("gx", "gy", None, None, None),
        ),
        out_specs=(P("gx", "gy", None, None), P(None, "gx", "gy", None)),
        check_vma=False,
    )
```

profile of v0, /device:TPU:12, one launch (start us, length us, event | category | flops | bytes accessed | tf_op | source)
XLA Modules:
  0.0 143.9 jit_solution(17450457453950254950)
XLA Ops:
  0.7 2.1 %collective-permute-start.8 = (f32[1,1,3,1024]{3,1,2,0:T(1,128)}, f32[1,1,3,1024]{3,1,2,0:T(1,128)S(1)}, u32[]{:S(2)}, u32[]{:S(2)}) collective-permute-start(f32[1,1,3,1024]{3,1,2,0:T(1,128)} %param.31), channel_id=1, source_target_pairs={{0,4},{4,8},{8,12},{12,16},{16,20},{20,24},{24,28},{1,5},{5,9},{9,... | collective-permute-start | bytes 36872 | tf_op jit(solution)/shard_map/ppermute | solution.py:37
  2.7 4.5 %collective-permute-start.9 = (f32[1,1,3,1024]{3,1,2,0:T(1,128)}, f32[1,1,3,1024]{3,1,2,0:T(1,128)S(1)}, u32[]{:S(2)}, u32[]{:S(2)}) collective-permute-start(f32[1,1,3,1024]{3,1,2,0:T(1,128)} %param.31), channel_id=1, source_target_pairs={{4,0},{8,4},{12,8},{16,12},{20,16},{24,20},{28,24},{5,1},{9,5},{13... | collective-permute-start | bytes 36872 | tf_op jit(solution)/shard_map/ppermute | solution.py:40
  10.9 3.1 %scatter_custom_fusion = s32[4,577]{0,1:T(8,128)S(1)} fusion(s32[1024]{0:T(1024)S(1)} %bitcast.292, s32[1024,4]{1,0:T(8,128)S(1)} %copy.50, s32[]{:T(128)} %constant.365.clone.1), kind=kCustom, calls=%fused_computation.173 | custom fusion | bytes 9236 | tf_op jit(solution)/shard_map/scatter | solution.py:171
  14.3 1.9 %collective-permute-start = (s32[1,3,4,64]{3,1,0,2:T(4,128)S(1)}, s32[1,3,4,64]{3,1,0,2:T(4,128)S(1)}, u32[]{:S(2)}, u32[]{:S(2)}) collective-permute-start(s32[1,3,4,64]{3,1,0,2:T(4,128)S(1)} %get-tuple-element.371), channel_id=1, source_target_pairs={{0,4},{4,8},{8,12},{12,16},{16,20},{20,24},{24,28},{1,5},{5,9},{9,... | collective-permute-start | bytes 9224 | tf_op jit(solution)/shard_map/ppermute | solution.py:37
  16.2 4.5 %collective-permute-start.1 = (s32[1,3,4,64]{3,1,0,2:T(4,128)S(1)}, s32[1,3,4,64]{3,1,0,2:T(4,128)S(1)}, u32[]{:S(2)}, u32[]{:S(2)}) collective-permute-start(s32[1,3,4,64]{3,1,0,2:T(4,128)S(1)} %get-tuple-element.372), channel_id=1, source_target_pairs={{4,0},{8,4},{12,8},{16,12},{20,16},{24,20},{28,24},{5,1},{9,5},{13... | collective-permute-start | bytes 9224 | tf_op jit(solution)/shard_map/ppermute | solution.py:40
  24.4 3.5 %collective-permute-start.2 = (s32[5,1,4,64]{3,1,0,2:T(1,128)S(1)}, s32[5,1,4,64]{3,1,0,2:T(1,128)S(1)}, u32[]{:S(2)}, u32[]{:S(2)}) collective-permute-start(s32[5,1,4,64]{3,1,0,2:T(1,128)S(1)} %get-tuple-element.339), channel_id=1, source_target_pairs={{0,1},{1,2},{2,3},{4,5},{5,6},{6,7},{8,9},{9,10},{10,11},{12,13},{... | collective-permute-start | bytes 15368 | tf_op jit(solution)/shard_map/ppermute | solution.py:37
  27.8 2.4 %collective-permute-start.3 = (s32[5,1,4,64]{3,1,0,2:T(1,128)S(1)}, s32[5,1,4,64]{3,1,0,2:T(1,128)S(1)}, u32[]{:S(2)}, u32[]{:S(2)}) collective-permute-start(s32[5,1,4,64]{3,1,0,2:T(1,128)S(1)} %get-tuple-element.340), channel_id=1, source_target_pairs={{1,0},{2,1},{3,2},{5,4},{6,5},{7,6},{9,8},{10,9},{11,10},{13,12},{... | collective-permute-start | bytes 15368 | tf_op jit(solution)/shard_map/ppermute | solution.py:40
  30.2 3.2 %collective-permute-done.3 = s32[5,1,4,64]{3,1,0,2:T(1,128)S(1)} collective-permute-done((s32[5,1,4,64]{3,1,0,2:T(1,128)S(1)}, s32[5,1,4,64]{3,1,0,2:T(1,128)S(1)}, u32[]{:S(2)}, u32[]{:S(2)}) %collective-permute-start.3) | collective-permute-done | bytes 5152 | tf_op jit(solution)/shard_map/ppermute | solution.py:40
  35.7 1.9 %collective-permute-start.4 = (bf16[1,3,6,64]{3,2,1,0:T(8,128)(2,1)S(1)}, bf16[1,3,6,64]{3,2,1,0:T(8,128)(2,1)S(1)}, u32[]{:S(2)}, u32[]{:S(2)}) collective-permute-start(bf16[1,3,6,64]{3,2,1,0:T(8,128)(2,1)S(1)} %get-tuple-element.373), channel_id=1, source_target_pairs={{0,4},{4,8},{8,12},{12,16},{16,20},{20,24},{24,28},{1,5},{5,9},{9,... | collective-permute-start | bytes 6920 | tf_op jit(solution)/shard_map/ppermute | solution.py:37
  37.6 4.5 %collective-permute-start.5 = (bf16[1,3,6,64]{3,2,1,0:T(8,128)(2,1)S(1)}, bf16[1,3,6,64]{3,2,1,0:T(8,128)(2,1)S(1)}, u32[]{:S(2)}, u32[]{:S(2)}) collective-permute-start(bf16[1,3,6,64]{3,2,1,0:T(8,128)(2,1)S(1)} %get-tuple-element.374), channel_id=1, source_target_pairs={{4,0},{8,4},{12,8},{16,12},{20,16},{24,20},{28,24},{5,1},{9,5},{13... | collective-permute-start | bytes 6920 | tf_op jit(solution)/shard_map/ppermute | solution.py:40
  42.7 0.8 collective-permute-done.5
  43.5 3.5 %collective-permute-start.6 = (bf16[5,1,6,64]{3,2,1,0:T(8,128)(2,1)S(1)}, bf16[5,1,6,64]{3,2,1,0:T(8,128)(2,1)S(1)}, u32[]{:S(2)}, u32[]{:S(2)}) collective-permute-start(bf16[5,1,6,64]{3,2,1,0:T(8,128)(2,1)S(1)} %get-tuple-element.365), channel_id=1, source_target_pairs={{0,1},{1,2},{2,3},{4,5},{5,6},{6,7},{8,9},{9,10},{10,11},{12,13},{... | collective-permute-start | bytes 11528 | tf_op jit(solution)/shard_map/ppermute | solution.py:37
  47.0 2.4 %collective-permute-start.7 = (bf16[5,1,6,64]{3,2,1,0:T(8,128)(2,1)S(1)}, bf16[5,1,6,64]{3,2,1,0:T(8,128)(2,1)S(1)}, u32[]{:S(2)}, u32[]{:S(2)}) collective-permute-start(bf16[5,1,6,64]{3,2,1,0:T(8,128)(2,1)S(1)} %get-tuple-element.366), channel_id=1, source_target_pairs={{1,0},{2,1},{3,2},{5,4},{6,5},{7,6},{9,8},{10,9},{11,10},{13,12},{... | collective-permute-start | bytes 11528 | tf_op jit(solution)/shard_map/ppermute | solution.py:40
  49.4 3.5 %collective-permute-start.10 = (f32[3,1,3,1024]{3,1,2,0:T(1,128)S(1)}, f32[3,1,3,1024]{3,1,2,0:T(1,128)S(1)}, u32[]{:S(2)}, u32[]{:S(2)}) collective-permute-start(f32[3,1,3,1024]{3,1,2,0:T(1,128)S(1)} %constant_dynamic-update-slice_fusion), channel_id=1, source_target_pairs={{0,1},{1,2},{2,3},{4,5},{5,6},{6,7},{8,9},{9,10},{10,11},{12,13},{... | collective-permute-start | bytes 110600 | tf_op jit(solution)/shard_map/ppermute | solution.py:37
  52.9 2.5 %collective-permute-start.11 = (f32[3,1,3,1024]{3,1,2,0:T(1,128)S(1)}, f32[3,1,3,1024]{3,1,2,0:T(1,128)S(1)}, u32[]{:S(2)}, u32[]{:S(2)}) collective-permute-start(f32[3,1,3,1024]{3,1,2,0:T(1,128)S(1)} %constant_dynamic-update-slice_fusion), channel_id=1, source_target_pairs={{1,0},{2,1},{3,2},{5,4},{6,5},{7,6},{9,8},{10,9},{11,10},{13,12},{... | collective-permute-start | bytes 110600 | tf_op jit(solution)/shard_map/ppermute | solution.py:40
  55.9 3.2 %gather_fusion = bf16[1024,6]{1,0:T(8,128)(2,1)S(1)} fusion(bf16[6,576]{0,1:T(8,128)(2,1)S(1)} %bitcast.212, s32[1024]{0:T(1024)S(1)} %broadcast_clamp_fusion), kind=kCustom, calls=%fused_computation | custom fusion | bytes 28672 | tf_op jit(solution)/shard_map/gather | solution.py:178
  59.7 37.9 %while.20 = (s32[]{:T(128)}, f32[2,3,512]{2,1,0:T(4,128)S(1)}, f32[2,3,512]{2,1,0:T(4,128)S(1)}, f32[3,1024]{1,0:T(4,128)S(1)}, f32[]{:T(128)}, /*index=5*/f32[3...) while((s32[]{:T(128)}, f32[2,3,512]{2,1,0:T(4,128)S(1)}, ...), condition=%wide.region_23.24_spmd, body=%wide.region_4.23_spmd.sunk | while | flops 94370304 | bytes 75886824 | solution.py:109
  59.7 1.8 %fusion.192 = (f32[512,1024]{1,0:T(8,128)S(1)}, f32[512,1024]{1,0:T(8,128)S(1)}) fusion(f32[3,1024]{1,0:T(4,128)S(1)} %get-tuple-element.656, f32[3,512]{1,0:T(4,128)S(1)} %dynamic-slice_bitcast_fusion.2, f32[3,1024]{1,0:T(4,128)S(1)} %get-tuple-element.654), kind=kLoop, calls=%fused_computation.22.clone.1 | loop fusion | flops 8388608 | bytes 4225024 | tf_op jit(solution)/shard_map/while/body/eval_jaxpr/reduce_sum | solution.py:103
  62.2 7.9 %fusion.193 = (f32[3,512]{1,0:T(4,128)S(1)}, f32[512,1024]{1,0:T(8,128)S(1)}, f32[512,1024]{1,0:T(8,128)S(1)}, f32[512,1024]{1,0:T(8,128)S(1)}, f32[512,1024]{1,...) fusion(f32[512,1024]{1,0:T(8,128)S(1)} %exponential_multiply_fu, ...), kind=kLoop, calls=%fused_computation.23.clone.1 | loop fusion | flops 38794240 | bytes 19003392 | tf_op jit(solution)/shard_map/while/body/eval_jaxpr/reduce_sum | solution.py:106
  70.2 1.0 exponential_multiply_fusion.20
  71.2 1.0 exponential_multiply_fusion.19
  72.1 1.0 exponential_multiply_fusion.18
  73.5 5.1 %fusion.194 = (f32[3,512]{1,0:T(4,128)S(1)}, f32[3,512]{1,0:T(4,128)S(1)}, f32[3,512]{1,0:T(4,128)S(1)}, f32[3,512]{1,0:T(4,128)S(1)}, f32[3,512]{1,0:T(4,128)S(...) fusion(f32[512,1024]{1,0:T(8,128)S(1)} %exponential_multiply_fusion.17, f32[3,1024]{1,0:T(4,128)S(1)} %get-tuple-element.658, ...), kind=kLoop, calls=%fused_computation.25.clone.1 | loop fusion | flops 33019392 | bytes 14815232 | tf_op jit(solution)/shard_map/while/body/eval_jaxpr/reduce_sum | solution.py:106
  78.6 1.8 %fusion.192 = (f32[512,1024]{1,0:T(8,128)S(1)}, f32[512,1024]{1,0:T(8,128)S(1)}) fusion(f32[3,1024]{1,0:T(4,128)S(1)} %get-tuple-element.656, f32[3,512]{1,0:T(4,128)S(1)} %dynamic-slice_bitcast_fusion.2, f32[3,1024]{1,0:T(4,128)S(1)} %get-tuple-element.654), kind=kLoop, calls=%fused_computation.22.clone.1 | loop fusion | flops 8388608 | bytes 4225024 | tf_op jit(solution)/shard_map/while/body/eval_jaxpr/reduce_sum | solution.py:103
  81.2 7.9 %fusion.193 = (f32[3,512]{1,0:T(4,128)S(1)}, f32[512,1024]{1,0:T(8,128)S(1)}, f32[512,1024]{1,0:T(8,128)S(1)}, f32[512,1024]{1,0:T(8,128)S(1)}, f32[512,1024]{1,...) fusion(f32[512,1024]{1,0:T(8,128)S(1)} %exponential_multiply_fu, ...), kind=kLoop, calls=%fused_computation.23.clone.1 | loop fusion | flops 38794240 | bytes 19003392 | tf_op jit(solution)/shard_map/while/body/eval_jaxpr/reduce_sum | solution.py:106
  89.1 1.0 exponential_multiply_fusion.20
  90.1 1.0 exponential_multiply_fusion.19
  91.0 1.0 exponential_multiply_fusion.18
  92.4 5.1 %fusion.194 = (f32[3,512]{1,0:T(4,128)S(1)}, f32[3,512]{1,0:T(4,128)S(1)}, f32[3,512]{1,0:T(4,128)S(1)}, f32[3,512]{1,0:T(4,128)S(1)}, f32[3,512]{1,0:T(4,128)S(...) fusion(f32[512,1024]{1,0:T(8,128)S(1)} %exponential_multiply_fusion.17, f32[3,1024]{1,0:T(4,128)S(1)} %get-tuple-element.658, ...), kind=kLoop, calls=%fused_computation.25.clone.1 | loop fusion | flops 33019392 | bytes 14815232 | tf_op jit(solution)/shard_map/while/body/eval_jaxpr/reduce_sum | solution.py:106
  98.5 1.9 %collective-permute-start.12 = (f32[1,1,4,1024]{3,2,1,0:T(4,128)S(1)}, f32[1,1,4,1024]{3,2,1,0:T(4,128)S(1)}, u32[]{:S(2)}, u32[]{:S(2)}) collective-permute-start(f32[1,1,4,1024]{3,2,1,0:T(4,128)S(1)} %fusion.188), channel_id=1, source_target_pairs={{0,4},{4,8},{8,12},{12,16},{16,20},{20,24},{24,28},{1,5},{5,9},{9,... | collective-permute-start | bytes 49160 | tf_op jit(solution)/shard_map/ppermute | solution.py:37
  100.4 4.8 %collective-permute-start.13 = (f32[1,1,4,1024]{3,2,1,0:T(4,128)S(1)}, f32[1,1,4,1024]{3,2,1,0:T(4,128)S(1)}, u32[]{:S(2)}, u32[]{:S(2)}) collective-permute-start(f32[1,1,4,1024]{3,2,1,0:T(4,128)S(1)} %fusion.188), channel_id=1, source_target_pairs={{4,0},{8,4},{12,8},{16,12},{20,16},{24,20},{28,24},{5,1},{9,5},{13... | collective-permute-start | bytes 49160 | tf_op jit(solution)/shard_map/ppermute | solution.py:40
  106.6 5.2 %fusion.20 = (f32[1024]{0:T(1024)}, f32[1024]{0:T(1024)S(1)}, f32[1024]{0:T(1024)S(1)}, f32[1024]{0:T(1024)S(1)}, f32[1024]{0:T(1024)S(1)}, /*index=5*/f32[1024]...) fusion(f32[1024]{0:T(1024)S(1)} %bitcast.280, f32[512]{0:T(512)S(1)} %add_multiply_fusion, ...), kind=kLoop, calls=%fused_computation.55 | loop fusion | flops 23583744 | bytes 75776 | tf_op jit(solution)/shard_map/reduce_sum | solution.py:66
  111.8 2.7 %fusion.19 = f32[4,256,512]{2,1,0:T(8,128)} fusion(f32[1024,256]{0,1:T(8,128)S(1)} %bitcast.211, f32[4,1024]{1,0:T(4,128)S(1)} %pad_maximum_fusion.11, f32[1024]{0:T(1024)S(1)} %get-tuple-element.256, f32[1024]{0:T(1024)S(1)} %bitcast.278, f32[512]{0:T(512)S(1)} %add_multiply_fusion), kind=kOutput, calls=%fused_computation.52 | convolution fusion | flops 1078984704 | bytes 3172352 | tf_op jit(solution)/shard_map/vtn,tl->vnl/dot_general | solution.py:86
  114.8 0.8 mul.1066
  116.2 0.8 copy.59
  117.0 3.5 %collective-permute-start.14 = (f32[3,1,4,1024]{3,2,1,0:T(4,128)S(1)}, f32[3,1,4,1024]{3,2,1,0:T(4,128)S(1)}, u32[]{:S(2)}, u32[]{:S(2)}) collective-permute-start(f32[3,1,4,1024]{3,2,1,0:T(4,128)S(1)} %pad_maximum_fusion.1), channel_id=1, source_target_pairs={{0,1},{1,2},{2,3},{4,5},{5,6},{6,7},{8,9},{9,10},{10,11},{12,13},{... | collective-permute-start | bytes 147464 | tf_op jit(solution)/shard_map/ppermute | solution.py:37
  120.5 2.4 %collective-permute-start.15 = (f32[3,1,4,1024]{3,2,1,0:T(4,128)S(1)}, f32[3,1,4,1024]{3,2,1,0:T(4,128)S(1)}, u32[]{:S(2)}, u32[]{:S(2)}) collective-permute-start(f32[3,1,4,1024]{3,2,1,0:T(4,128)S(1)} %pad_maximum_fusion.1), channel_id=1, source_target_pairs={{1,0},{2,1},{3,2},{5,4},{6,5},{7,6},{9,8},{10,9},{11,10},{13,12},{... | collective-permute-start | bytes 147464 | tf_op jit(solution)/shard_map/ppermute | solution.py:40
  122.9 0.8 fusion.49
  123.7 1.6 %fusion.43 = f32[4,64,512]{2,1,0:T(8,128)} fusion(f32[1024]{0:T(1024)S(1)} %get-tuple-element.259, f32[1024]{0:T(1024)S(1)} %bitcast.294, f32[512]{0:T(512)S(1)} %add_multiply_fusion, f32[1024,64]{0,1:T(8,128)S(1)} %bitcast.219, f32[4,1024]{1,0:T(4,128)S(1)} %bitcast.274), kind=kOutput, calls=%fused_computation.97 | convolution fusion | flops 272105472 | bytes 813056 | tf_op jit(solution)/shard_map/vtn,tl->vnl/dot_general | solution.py:86
  125.2 0.8 fusion.47
  126.5 1.4 fusion.75
  129.1 1.9 %add_select_fusion = f32[4,4,4,512]{3,2,1,0:T(4,128)S(1)} fusion(f32[4,4,4,512]{3,2,1,0:T(4,128)S(1)} %reshape.1716, f32[4,16,16,512]{3,2,1,0:T(8,128)S(1)} %fusion.80, s32[]{:T(128)} %bitcast.75, s32[]{:T(128)} %bitcast.76, pred[]{:T(512)} %and_reduce_fusion), kind=kLoop, calls=%fused_computation.166 | loop fusion | flops 65536 | bytes 393225 | tf_op jit(solution)/shard_map/select.11
  131.0 1.6 %scatter-add.30 = f32[4,16,16,512]{3,2,1,0:T(8,128)S(1)} dynamic-update-slice(f32[4,16,16,512]{3,2,1,0:T(8,128)S(1)} %fusion.80, f32[4,4,4,512]{3,2,1,0:T(4,128)S(1)} %add_select_fusion, s32[]{:T(128)} %constant.365.clone.1, s32[]{:T(128)} %bitcast.75, s32[]{:T(128)} %bitcast.76, s32[]{:T(128)} %constant.365.clone.1) | dynamic-update-slice | bytes 262148 | tf_op jit(solution)/shard_map/scatter-add | solution.py:215
  132.6 2.5 %fusion.45 = f32[4,64,512]{2,1,0:T(8,128)} fusion(f32[1024]{0:T(1024)S(1)} %copy-done.19, f32[1024]{0:T(1024)S(1)} %bitcast.283, f32[512]{0:T(512)S(1)} %copy-done.16, f32[1024,64]{0,1:T(8,128)} %mul.1066, f32[4,1024]{1,0:T(4,128)S(1)} %get-tuple-element.334), kind=kOutput, calls=%fused_computation.98 | convolution fusion | flops 272105472 | bytes 813056 | tf_op jit(solution)/shard_map/vtn,tl->vnl/dot_general | solution.py:86
  135.1 1.2 reshape.1719
  137.1 1.5 %fusion.71 = f32[4,16,512]{2,1,0:T(8,128)S(1)} fusion(f32[1024]{0:T(1024)} %get-tuple-element.252, f32[1024]{0:T(1024)} %bitcast.281, f32[512]{0:T(512)} %copy-done.14, f32[1024,16]{0,1:T(8,128)} %mul.1102, f32[4,1024]{1,0:T(4,128)S(1)} %get-tuple-element.333), kind=kOutput, calls=%fused_computation.127 | convolution fusion | flops 70385664 | bytes 223232 | tf_op jit(solution)/shard_map/vtn,tl->vnl/dot_general | solution.py:86
  138.9 2.1 %add.1056 = f32[4,16,16,512]{3,2,1,0:T(8,128)S(1)} add(f32[4,16,16,512]{3,2,1,0:T(8,128)S(1)} %fusion.82, f32[4,16,16,512]{3,2,1,0:T(8,128)} %bitcast.209) | non-fusion elementwise | flops 524288 | bytes 6291456 | tf_op jit(solution)/shard_map/add | solution.py:215
  142.3 1.6 %broadcast_multiply_fusion = f32[4,16,16,512]{3,2,1,0:T(8,128)} fusion(f32[4,16,16,512]{3,2,1,0:T(8,128)S(1)} %fusion.103), kind=kLoop, calls=%fused_computation.101 | loop fusion | flops 524288 | bytes 4194304 | tf_op jit(solution)/shard_map/mul | solution.py:218
  (194 shorter events, 19.9 us)
Async XLA Ops:
  0.6 20.5 %copy-start = (f32[64,8]{1,0:T(8,128)S(1)}, f32[64,8]{1,0:T(8,128)}, u32[]{:S(2)}) copy-start(f32[64,8]{1,0:T(8,128)} %constant.391.clone) | copy-start | bytes 6148
  0.6 20.1 %copy-start.4 = (f32[1,1,3,1024]{3,1,2,0:T(1,128)S(1)}, f32[1,1,3,1024]{3,1,2,0:T(1,128)}, u32[]{:S(2)}) copy-start(f32[1,1,3,1024]{3,1,2,0:T(1,128)} %param.31) | copy-start | bytes 36868
  0.7 20.1 %copy-start.3 = (s32[1,1,3,1024]{3,1,2,0:T(1,128)S(1)}, s32[1,1,3,1024]{3,1,2,0:T(1,128)}, u32[]{:S(2)}) copy-start(s32[1,1,3,1024]{3,1,2,0:T(1,128)} %param.37) | copy-start | bytes 36868
  0.7 20.2 %copy-start.2 = (bf16[1,1,32,6,512]{4,2,3,1,0:T(8,128)(2,1)S(1)}, bf16[1,1,32,6,512]{4,2,3,1,0:T(8,128)(2,1)}, u32[]{:S(2)}) copy-start(bf16[1,1,32,6,512]{4,2,3,1,0:T(8,128)(2,1)} %param.38) | copy-start | bytes 589828
  0.7 48.7 %collective-permute-start.8 = (f32[1,1,3,1024]{3,1,2,0:T(1,128)}, f32[1,1,3,1024]{3,1,2,0:T(1,128)S(1)}, u32[]{:S(2)}, u32[]{:S(2)}) collective-permute-start(f32[1,1,3,1024]{3,1,2,0:T(1,128)} %param.31), channel_id=1, source_target_pairs={{0,4},{4,8},{8,12},{12,16},{16,20},{20,24},{24,28},{1,5},{5,9},{9,... | collective-permute-start | bytes 36872 | tf_op jit(solution)/shard_map/ppermute | solution.py:37
  2.7 46.6 %collective-permute-start.9 = (f32[1,1,3,1024]{3,1,2,0:T(1,128)}, f32[1,1,3,1024]{3,1,2,0:T(1,128)S(1)}, u32[]{:S(2)}, u32[]{:S(2)}) collective-permute-start(f32[1,1,3,1024]{3,1,2,0:T(1,128)} %param.31), channel_id=1, source_target_pairs={{4,0},{8,4},{12,8},{16,12},{20,16},{24,20},{28,24},{5,1},{9,5},{13... | collective-permute-start | bytes 36872 | tf_op jit(solution)/shard_map/ppermute | solution.py:40
  14.3 10.1 %collective-permute-start = (s32[1,3,4,64]{3,1,0,2:T(4,128)S(1)}, s32[1,3,4,64]{3,1,0,2:T(4,128)S(1)}, u32[]{:S(2)}, u32[]{:S(2)}) collective-permute-start(s32[1,3,4,64]{3,1,0,2:T(4,128)S(1)} %get-tuple-element.371), channel_id=1, source_target_pairs={{0,4},{4,8},{8,12},{12,16},{16,20},{20,24},{24,28},{1,5},{5,9},{9,... | collective-permute-start | bytes 9224 | tf_op jit(solution)/shard_map/ppermute | solution.py:37
  16.2 8.1 %collective-permute-start.1 = (s32[1,3,4,64]{3,1,0,2:T(4,128)S(1)}, s32[1,3,4,64]{3,1,0,2:T(4,128)S(1)}, u32[]{:S(2)}, u32[]{:S(2)}) collective-permute-start(s32[1,3,4,64]{3,1,0,2:T(4,128)S(1)} %get-tuple-element.372), channel_id=1, source_target_pairs={{4,0},{8,4},{12,8},{16,12},{20,16},{24,20},{28,24},{5,1},{9,5},{13... | collective-permute-start | bytes 9224 | tf_op jit(solution)/shard_map/ppermute | solution.py:40
  20.8 104.4 %copy-start.14 = (f32[512]{0:T(512)}, f32[512]{0:T(512)S(1)}, u32[]{:S(2)}) copy-start(f32[512]{0:T(512)S(1)} %add_multiply_fusion) | copy-start | bytes 6148
  22.0 0.7 copy-start.6
  22.0 1.5 %copy-start.17 = (s32[4]{0:T(128)S(1)}, s32[4]{0:T(128)}, u32[]{:S(2)}) copy-start(s32[4]{0:T(128)} %constant.388.clone.1) | copy-start | bytes 52
  24.4 5.9 %collective-permute-start.2 = (s32[5,1,4,64]{3,1,0,2:T(1,128)S(1)}, s32[5,1,4,64]{3,1,0,2:T(1,128)S(1)}, u32[]{:S(2)}, u32[]{:S(2)}) collective-permute-start(s32[5,1,4,64]{3,1,0,2:T(1,128)S(1)} %get-tuple-element.339), channel_id=1, source_target_pairs={{0,1},{1,2},{2,3},{4,5},{5,6},{6,7},{8,9},{9,10},{10,11},{12,13},{... | collective-permute-start | bytes 15368 | tf_op jit(solution)/shard_map/ppermute | solution.py:37
  27.8 5.6 %collective-permute-start.3 = (s32[5,1,4,64]{3,1,0,2:T(1,128)S(1)}, s32[5,1,4,64]{3,1,0,2:T(1,128)S(1)}, u32[]{:S(2)}, u32[]{:S(2)}) collective-permute-start(s32[5,1,4,64]{3,1,0,2:T(1,128)S(1)} %get-tuple-element.340), channel_id=1, source_target_pairs={{1,0},{2,1},{3,2},{5,4},{6,5},{7,6},{9,8},{10,9},{11,10},{13,12},{... | collective-permute-start | bytes 15368 | tf_op jit(solution)/shard_map/ppermute | solution.py:40
  34.9 7.5 %copy-start.7 = (f32[1,1,3,1024]{3,1,2,0:T(1,128)S(1)}, f32[1,1,3,1024]{3,1,2,0:T(1,128)}, u32[]{:S(2)}) copy-start(f32[1,1,3,1024]{3,1,2,0:T(1,128)} %param.32) | copy-start | bytes 36868
  35.7 7.0 %collective-permute-start.4 = (bf16[1,3,6,64]{3,2,1,0:T(8,128)(2,1)S(1)}, bf16[1,3,6,64]{3,2,1,0:T(8,128)(2,1)S(1)}, u32[]{:S(2)}, u32[]{:S(2)}) collective-permute-start(bf16[1,3,6,64]{3,2,1,0:T(8,128)(2,1)S(1)} %get-tuple-element.373), channel_id=1, source_target_pairs={{0,4},{4,8},{8,12},{12,16},{16,20},{20,24},{24,28},{1,5},{5,9},{9,... | collective-permute-start | bytes 6920 | tf_op jit(solution)/shard_map/ppermute | solution.py:37
  37.6 5.9 %collective-permute-start.5 = (bf16[1,3,6,64]{3,2,1,0:T(8,128)(2,1)S(1)}, bf16[1,3,6,64]{3,2,1,0:T(8,128)(2,1)S(1)}, u32[]{:S(2)}, u32[]{:S(2)}) collective-permute-start(bf16[1,3,6,64]{3,2,1,0:T(8,128)(2,1)S(1)} %get-tuple-element.374), channel_id=1, source_target_pairs={{4,0},{8,4},{12,8},{16,12},{20,16},{24,20},{28,24},{5,1},{9,5},{13... | collective-permute-start | bytes 6920 | tf_op jit(solution)/shard_map/ppermute | solution.py:40
  43.5 12.2 %collective-permute-start.6 = (bf16[5,1,6,64]{3,2,1,0:T(8,128)(2,1)S(1)}, bf16[5,1,6,64]{3,2,1,0:T(8,128)(2,1)S(1)}, u32[]{:S(2)}, u32[]{:S(2)}) collective-permute-start(bf16[5,1,6,64]{3,2,1,0:T(8,128)(2,1)S(1)} %get-tuple-element.365), channel_id=1, source_target_pairs={{0,1},{1,2},{2,3},{4,5},{5,6},{6,7},{8,9},{9,10},{10,11},{12,13},{... | collective-permute-start | bytes 11528 | tf_op jit(solution)/shard_map/ppermute | solution.py:37
  47.0 8.8 %collective-permute-start.7 = (bf16[5,1,6,64]{3,2,1,0:T(8,128)(2,1)S(1)}, bf16[5,1,6,64]{3,2,1,0:T(8,128)(2,1)S(1)}, u32[]{:S(2)}, u32[]{:S(2)}) collective-permute-start(bf16[5,1,6,64]{3,2,1,0:T(8,128)(2,1)S(1)} %get-tuple-element.366), channel_id=1, source_target_pairs={{1,0},{2,1},{3,2},{5,4},{6,5},{7,6},{9,8},{10,9},{11,10},{13,12},{... | collective-permute-start | bytes 11528 | tf_op jit(solution)/shard_map/ppermute | solution.py:40
  49.4 10.1 %collective-permute-start.10 = (f32[3,1,3,1024]{3,1,2,0:T(1,128)S(1)}, f32[3,1,3,1024]{3,1,2,0:T(1,128)S(1)}, u32[]{:S(2)}, u32[]{:S(2)}) collective-permute-start(f32[3,1,3,1024]{3,1,2,0:T(1,128)S(1)} %constant_dynamic-update-slice_fusion), channel_id=1, source_target_pairs={{0,1},{1,2},{2,3},{4,5},{5,6},{6,7},{8,9},{9,10},{10,11},{12,13},{... | collective-permute-start | bytes 110600 | tf_op jit(solution)/shard_map/ppermute | solution.py:37
  52.9 6.5 %collective-permute-start.11 = (f32[3,1,3,1024]{3,1,2,0:T(1,128)S(1)}, f32[3,1,3,1024]{3,1,2,0:T(1,128)S(1)}, u32[]{:S(2)}, u32[]{:S(2)}) collective-permute-start(f32[3,1,3,1024]{3,1,2,0:T(1,128)S(1)} %constant_dynamic-update-slice_fusion), channel_id=1, source_target_pairs={{1,0},{2,1},{3,2},{5,4},{6,5},{7,6},{9,8},{10,9},{11,10},{13,12},{... | collective-permute-start | bytes 110600 | tf_op jit(solution)/shard_map/ppermute | solution.py:40
  59.4 47.2 %copy-start.9 = (f32[1,1,1,1024]{3,1,2,0:T(1,128)}, f32[1,1,1,1024]{3,1,2,0:T(1,128)S(1)}, u32[]{:S(2)}) copy-start(f32[1,1,1,1024]{3,1,2,0:T(1,128)S(1)} %get-tuple-element.357) | copy-start | bytes 12292
  59.4 47.2 %copy-start.10 = (f32[1,1,1,1024]{3,1,2,0:T(1,128)}, f32[1,1,1,1024]{3,1,2,0:T(1,128)S(1)}, u32[]{:S(2)}) copy-start(f32[1,1,1,1024]{3,1,2,0:T(1,128)S(1)} %get-tuple-element.353) | copy-start | bytes 12292
  59.5 47.1 %copy-start.12 = (f32[1,1,1,1024]{3,1,2,0:T(1,128)}, f32[1,1,1,1024]{3,1,2,0:T(1,128)S(1)}, u32[]{:S(2)}) copy-start(f32[1,1,1,1024]{3,1,2,0:T(1,128)S(1)} %get-tuple-element.345) | copy-start | bytes 12292
  59.7 38.1 %copy-start.5 = (f32[1,1,1024]{2,1,0:T(1,128)S(1)}, f32[1,1,1024]{2,1,0:T(1,128)}, u32[]{:S(2)}) copy-start(f32[1,1,1024]{2,1,0:T(1,128)} %param.34) | copy-start | bytes 12292
  59.7 38.1 %copy-start.8 = (f32[1,1,1024]{2,1,0:T(1,128)S(1)}, f32[1,1,1024]{2,1,0:T(1,128)}, u32[]{:S(2)}) copy-start(f32[1,1,1024]{2,1,0:T(1,128)} %param.33) | copy-start | bytes 12292
  98.5 18.5 %collective-permute-start.12 = (f32[1,1,4,1024]{3,2,1,0:T(4,128)S(1)}, f32[1,1,4,1024]{3,2,1,0:T(4,128)S(1)}, u32[]{:S(2)}, u32[]{:S(2)}) collective-permute-start(f32[1,1,4,1024]{3,2,1,0:T(4,128)S(1)} %fusion.188), channel_id=1, source_target_pairs={{0,4},{4,8},{8,12},{12,16},{16,20},{20,24},{24,28},{1,5},{5,9},{9,... | collective-permute-start | bytes 49160 | tf_op jit(solution)/shard_map/ppermute | solution.py:37
  100.4 16.6 %collective-permute-start.13 = (f32[1,1,4,1024]{3,2,1,0:T(4,128)S(1)}, f32[1,1,4,1024]{3,2,1,0:T(4,128)S(1)}, u32[]{:S(2)}, u32[]{:S(2)}) collective-permute-start(f32[1,1,4,1024]{3,2,1,0:T(4,128)S(1)} %fusion.188), channel_id=1, source_target_pairs={{4,0},{8,4},{12,8},{16,12},{20,16},{24,20},{28,24},{5,1},{9,5},{13... | collective-permute-start | bytes 49160 | tf_op jit(solution)/shard_map/ppermute | solution.py:40
  117.0 8.2 %collective-permute-start.14 = (f32[3,1,4,1024]{3,2,1,0:T(4,128)S(1)}, f32[3,1,4,1024]{3,2,1,0:T(4,128)S(1)}, u32[]{:S(2)}, u32[]{:S(2)}) collective-permute-start(f32[3,1,4,1024]{3,2,1,0:T(4,128)S(1)} %pad_maximum_fusion.1), channel_id=1, source_target_pairs={{0,1},{1,2},{2,3},{4,5},{5,6},{6,7},{8,9},{9,10},{10,11},{12,13},{... | collective-permute-start | bytes 147464 | tf_op jit(solution)/shard_map/ppermute | solution.py:37
  120.5 6.0 %collective-permute-start.15 = (f32[3,1,4,1024]{3,2,1,0:T(4,128)S(1)}, f32[3,1,4,1024]{3,2,1,0:T(4,128)S(1)}, u32[]{:S(2)}, u32[]{:S(2)}) collective-permute-start(f32[3,1,4,1024]{3,2,1,0:T(4,128)S(1)} %pad_maximum_fusion.1), channel_id=1, source_target_pairs={{1,0},{2,1},{3,2},{5,4},{6,5},{7,6},{9,8},{10,9},{11,10},{13,12},{... | collective-permute-start | bytes 147464 | tf_op jit(solution)/shard_map/ppermute | solution.py:40
  126.5 1.5 %copy-start.15 = (f32[512]{0:T(512)S(1)}, f32[512]{0:T(512)}, u32[]{:S(2)}) copy-start(f32[512]{0:T(512)} %copy-done.14) | copy-start | bytes 6148
  128.7 3.8 %copy-start.11 = (f32[1,1,1,1024]{3,1,2,0:T(1,128)S(1)}, f32[1,1,1,1024]{3,1,2,0:T(1,128)}, u32[]{:S(2)}) copy-start(f32[1,1,1,1024]{3,1,2,0:T(1,128)} %copy-done.10) | copy-start | bytes 12292
  128.8 3.8 %copy-start.16 = (f32[512]{0:T(512)S(1)}, f32[512]{0:T(512)}, u32[]{:S(2)}) copy-start(f32[512]{0:T(512)} %copy-done.14) | copy-start | bytes 6148
  128.8 3.8 %copy-start.19 = (f32[1024]{0:T(1024)S(1)}, f32[1024]{0:T(1024)}, u32[]{:S(2)}) copy-start(f32[1024]{0:T(1024)} %get-tuple-element.257) | copy-start | bytes 12292
  132.6 3.7 %copy-start.13 = (f32[1,1,1,1024]{3,1,2,0:T(1,128)S(1)}, f32[1,1,1,1024]{3,1,2,0:T(1,128)}, u32[]{:S(2)}) copy-start(f32[1,1,1,1024]{3,1,2,0:T(1,128)} %copy-done.12) | copy-start | bytes 12292
  132.6 3.7 %copy-start.18 = (f32[1024]{0:T(1024)S(1)}, f32[1024]{0:T(1024)}, u32[]{:S(2)}) copy-start(f32[1024]{0:T(1024)} %get-tuple-element.258) | copy-start | bytes 12292
  141.0 1.0 copy-start.1
where the time goes:
time: 145 us; the launch traced here: 144 us
  other arithmetic  55.4 us (38%)
  starting transfers between devices  49.7 us (34%)
  local copies, waits for them, and re-layouts  17 us (12%)
  matrix products  15.2 us (10%)
  waiting for transfers between devices  4.34 us (3%)
  between operations  1.99 us (1%)
    ppermute x8, starting transfers between devices, padded(): lax.ppermute(lax.slice_in_dim(block, 0, width, axis=dim), axis, backward)  28 us
    reduce_sum x4, other arithmetic, one_group(): summed = summed + jnp.sum(offset * closeness[None, :, :], axis=2)  26 us
    ppermute x8, starting transfers between devices, padded(): lax.ppermute(lax.slice_in_dim(block, block.shape[dim] - width, None, axis...  21.8 us
    dot_general x9, matrix products, window_cube(): jnp.einsum('vtn,tl->vnl', scattered_loads, along_depth, preferred_element...  12.7 us
    mul x12, other arithmetic, one_group(): jnp.exp(-jnp.sum(offset * offset, axis=0) / (2.0 * PAIR_WIDTH * PAIR_WIDTH))  7.98 us
    reduce_sum x7, other arithmetic, gaussian_rows(): return bumps / jnp.sum(bumps, axis=1, keepdims=True)  6.11 us
    ppermute x8, waiting for transfers between devices, padded(): lax.ppermute(lax.slice_in_dim(block, 0, width, axis=dim), axis, backward)  4.32 us
    reduce_sum x2, other arithmetic, one_group(): jnp.sum(offset * offset, axis=0)  3.62 us
  transfers between devices with their start and end apart: 16, of which 3 were waited for; matrix products, arithmetic and copies ran while one was open for 22% of the time, Pallas kernels for 0%

commit v1 on v0

v1 whole, which is shorter than its diff:
```python
import math
from functools import partial

import jax
import jax.numpy as jnp
import numpy as np
from jax import lax
from jax.experimental import pallas as pl
from jax.experimental.pallas import tpu as pltpu
from jax.sharding import PartitionSpec as P

BX = 16
BY = 16
MARGIN = 4
QUANT = 64
CAP = 64
NODES = 8

GLL_NODES = (
    -1.0,
    -0.8717401485096066,
    -0.5917001814331423,
    -0.2092992179024789,
    0.2092992179024789,
    0.5917001814331423,
    0.8717401485096066,
    1.0,
)
STIFFNESS = 0.5
PAIR_WIDTH = 0.3
FILTER_BINS = 3.0

F32 = jnp.float32
BF16 = jnp.bfloat16
VMEM = pl.BlockSpec(memory_space=pltpu.VMEM)
PAIR_SCALE = math.sqrt(math.log2(math.e)) / PAIR_WIDTH
FILTER_SCALE = math.sqrt(0.5 * math.log2(math.e)) / FILTER_BINS
NEVER = -1e30


def basis_table(levels):
    points = -1.0 + (2.0 * np.arange(levels) + 1.0) / levels
    lagrange = np.ones((levels, NODES))
    for node_a in range(NODES):
        for node_b in range(NODES):
            if node_b != node_a:
                lagrange[:, node_a] *= (points - GLL_NODES[node_b]) / (
                    GLL_NODES[node_a] - GLL_NODES[node_b]
                )
    return lagrange.astype(np.float32)


def split_table():
    table = basis_table(QUANT).T
    parts = []
    for _ in range(3):
        head = table.astype(jnp.bfloat16)
        parts.append(head)
        table = table - head.astype(np.float32)
    return np.concatenate(parts, axis=0)


def split3(values):
    first = values.astype(BF16).astype(F32)
    rest = values - first
    second = rest.astype(BF16).astype(F32)
    return first, second, rest - second


def partner(axis, which):
    index = lax.axis_index(axis)
    step = 1 - 2 * lax.rem(index, 2)
    if which:
        step = -step
    there = index + step
    return step, (there >= 0) & (there < lax.axis_size(axis))


def swap(block, axis, which):
    count = lax.axis_size(axis)
    pairs = [(i, i + 1) for i in range(which, count - 1, 2)]
    return lax.ppermute(block, axis, pairs + [(b, a) for a, b in pairs])


def features(block, step_x, step_y, present, half_depth):
    row = lax.broadcasted_iota(jnp.int32, block.shape, 0)
    scale = jnp.where(row == 2, 2.0 * half_depth * PAIR_SCALE, PAIR_SCALE)
    shift = jnp.where(
        row == 0,
        (step_x.astype(F32) - 0.5) * PAIR_SCALE,
        jnp.where(row == 1, (step_y.astype(F32) - 0.5) * PAIR_SCALE, -half_depth * PAIR_SCALE),
    )
    place = jnp.where(row < 3, block * scale + shift, 0.0)
    norm = -0.5 * jnp.sum(place * place, axis=0, keepdims=True)
    norm = jnp.where(present, norm, NEVER)
    source = jnp.where(row == 3, norm, jnp.where(row == 4, 1.0, place))
    target = jnp.where(row == 3, 1.0, jnp.where(row == 4, norm, place))
    return place, source, target


def target_rows(own, half_depth):
    place, _, target = features(own, jnp.int32(0), jnp.int32(0), True, half_depth)
    a, b, c = split3(target)
    return place, jnp.concatenate([a, b, a, b, c, a], axis=0).astype(BF16)


def depth_centres(depth):
    return (lax.broadcasted_iota(jnp.int32, (1, depth), 1).astype(F32) + 0.5) * FILTER_SCALE


def depth_column(block, depth):
    return jnp.transpose(block[0:8] * (depth * FILTER_SCALE))[:, 2:3]


def depth_rows(column, depth):
    distance = column - depth_centres(depth)
    bumps = jnp.exp2(-(distance * distance))
    return (bumps * (1.0 / jnp.sum(bumps, axis=1, keepdims=True))).astype(BF16)


def pair_block(block, step_x, step_y, present, half_depth, target_ref, total_ref, depth_ref):
    particles = block.shape[1]
    depth = depth_ref.shape[1]
    column = depth_column(block, depth)
    _, source, _ = features(block, step_x, step_y, present, half_depth)
    a, b, c = split3(source)
    rows = jnp.concatenate([a, a, b, b, a, c], axis=0).astype(BF16)
    values = jnp.concatenate([a, b, c, jnp.zeros_like(a)], axis=0).astype(BF16)
    width = min(256, particles)
    for start in range(0, particles, width):
        exponent = lax.dot_general(
            rows,
            target_ref[:, start : start + width],
            (((0,), (0,)), ((), ())),
            preferred_element_type=F32,
        )
        weight = jnp.exp2(exponent)
        high = weight.astype(BF16)
        low = (weight - high.astype(F32)).astype(BF16)
        sums = jnp.dot(values, high, preferred_element_type=F32) + jnp.dot(
            values, low, preferred_element_type=F32
        )
        total_ref[:, start : start + width] += sums[0:8] + sums[8:16] + sums[16:24]
        depth_ref[start : start + width] = depth_rows(column[start : start + width], depth)


def y_steps():
    step_a, has_a = partner("gy", 0)
    step_b, has_b = partner("gy", 1)
    return ((step_a, has_a), (jnp.int32(0), jnp.bool_(True)), (step_b, has_b))


def interpolate(request, table_ref, basis_ref, weight_ref):
    slots = request.shape[1]
    elements = table_ref.shape[0] // 6
    level = lax.broadcasted_iota(jnp.int32, (QUANT, slots), 0).astype(F32)
    factors = []
    for axis in range(3):
        chosen = jnp.where(level == request[1 + axis : 2 + axis], 1.0, 0.0).astype(BF16)
        parts = jnp.dot(basis_ref[...], chosen, preferred_element_type=F32)
        factors.append(parts[0:8] + (parts[8:16] + parts[16:24]))
    for a in range(NODES):
        first = factors[0][a : a + 1] * factors[1]
        for b in range(0, NODES, 2):
            pair = jnp.concatenate(
                [first[b : b + 1] * factors[2], first[b + 1 : b + 2] * factors[2]], axis=0
            )
            start = (a * NODES + b) * NODES
            weight_ref[start : start + 2 * NODES, :slots] = pair.astype(BF16)
    projected = jnp.dot(table_ref[...], weight_ref[:, :slots], preferred_element_type=F32)
    local = lax.broadcasted_iota(jnp.int32, (elements, slots), 0).astype(F32)
    picked = jnp.where(local == request[0:1], 1.0, 0.0)
    rows = [
        jnp.sum(projected[k * elements : (k + 1) * elements] * picked, axis=0, keepdims=True)
        for k in range(6)
    ]
    return jnp.concatenate(rows + [jnp.zeros((2, slots), F32)], axis=0)


def my_flat():
    return (lax.axis_index("gx") * lax.axis_size("gy") + lax.axis_index("gy")).astype(F32)


def pack_kernel(fractions_ref, owner_ref, element_ref, coords_ref, out_ref):
    for k in range(3):
        out_ref[k : k + 1] = fractions_ref[k]
        out_ref[5 + k : 6 + k] = coords_ref[k].astype(F32)
    out_ref[3:4] = owner_ref[...].astype(F32)
    out_ref[4:5] = element_ref[...].astype(F32)


def own_kernel(
    half_depth, own_ref, far_table_ref, far_basis_ref, total_ref, values_ref, depth_ref,
    target_ref, weight_ref, table_ref, basis_ref, arrived,
):
    fetches = [
        pltpu.make_async_copy(far_table_ref, table_ref, arrived.at[0]),
        pltpu.make_async_copy(far_basis_ref, basis_ref, arrived.at[1]),
    ]
    for fetch in fetches:
        fetch.start()
    own = own_ref[...]
    _, target = target_rows(own, half_depth)
    target_ref[...] = target
    total_ref[...] = jnp.zeros_like(total_ref)
    zero = jnp.int32(0)
    pair_block(own, zero, zero, True, half_depth, target_ref, total_ref, depth_ref)
    for fetch in fetches:
        fetch.wait()
    values = interpolate(own[4:8], table_ref, basis_ref, weight_ref)
    values_ref[...] = jnp.where(own[3:4] == my_flat(), values, 0.0).astype(BF16)


def column_kernel(
    half_depth, own_ref, first_ref, second_ref, sum_ref, total_ref, depth_ref, target_ref
):
    _, target = target_rows(own_ref[...], half_depth)
    target_ref[...] = target
    total_ref[...] = sum_ref[...]
    steps = y_steps()
    zero = jnp.int32(0)
    for n, (ref, (step, present)) in enumerate(((first_ref, steps[0]), (second_ref, steps[2]))):
        pair_block(ref[...], zero, step, present, half_depth, target_ref, total_ref, depth_ref.at[n])


def side_kernel(
    which, half_depth, own_ref, blocks_ref, sum_ref, total_ref, depth_ref, target_ref
):
    _, target = target_rows(own_ref[...], half_depth)
    target_ref[...] = target
    total_ref[...] = sum_ref[...]
    step_x, has_x = partner("gx", which)
    for k, (step, present) in enumerate(y_steps()):
        pair_block(
            blocks_ref[k], step_x, step, present & has_x, half_depth, target_ref, total_ref,
            depth_ref.at[k],
        )


def serve_kernel(
    za_ref, zb_ref, xa_ref, xb_ref, table_ref, basis_ref,
    zout_ref, xaout_ref, xbout_ref, chosen_ref, weight_ref,
):
    particles = za_ref.shape[1]
    steps = y_steps()
    _, has_a = partner("gx", 0)
    _, has_b = partner("gx", 1)
    blocks = [(za_ref[...], steps[0][1], (zout_ref, 0)), (zb_ref[...], steps[2][1], (zout_ref, 1))]
    for ref, out, has in ((xa_ref, xaout_ref, has_a), (xb_ref, xbout_ref, has_b)):
        for k in range(3):
            blocks.append((ref[k], steps[k][1] & has, (out, k)))
    me = my_flat()
    mask = jnp.concatenate(
        [jnp.where((b[3:4] == me) & present, 1.0, 0.0) for b, present, _ in blocks], axis=0
    )
    lanes = 128
    chunks = particles // lanes
    upper = jnp.where(
        lax.broadcasted_iota(jnp.int32, (lanes, lanes), 0)
        < lax.broadcasted_iota(jnp.int32, (lanes, lanes), 1),
        1.0,
        0.0,
    ).astype(BF16)
    stacked = jnp.concatenate([mask[:, j * lanes : (j + 1) * lanes] for j in range(chunks)], axis=0)
    inside = jnp.dot(stacked.astype(BF16), upper, preferred_element_type=F32)
    counts = jnp.sum(stacked, axis=1, keepdims=True)
    before = jnp.zeros((8, 1), F32)
    ranks = []
    for j in range(chunks):
        ranks.append(inside[8 * j : 8 * j + 8] + before)
        before = before + counts[8 * j : 8 * j + 8]
    rank = jnp.concatenate(ranks, axis=1)
    slot = lax.broadcasted_iota(jnp.int32, (2 * CAP, particles), 0).astype(F32)
    requests = []
    for pair in range(4):
        part = jnp.zeros((8, 2 * CAP), F32)
        for half in range(2):
            b = 2 * pair + half
            place = jnp.where(mask[b : b + 1] > 0.0, rank[b : b + 1] + half * CAP, -1.0)
            chosen = jnp.where(slot == place, 1.0, 0.0).astype(BF16)
            chosen_ref[b] = chosen
            part = part + lax.dot_general(
                blocks[b][0].astype(BF16), chosen, (((1,), (1,)), ((), ())), preferred_element_type=F32
            )
        requests.append(part)
    request = jnp.concatenate(requests, axis=1)
    values = interpolate(request[4:8], table_ref, basis_ref, weight_ref).astype(BF16)
    for b, (_, _, (out, k)) in enumerate(blocks):
        reply = values[:, (b // 2) * 2 * CAP : (b // 2 + 1) * 2 * CAP]
        out[k] = jnp.dot(reply, chosen_ref[b], preferred_element_type=F32).astype(BF16)


def join_kernel(own_ref, z_ref, xa_ref, xb_ref, mid_ref, za_ref, zb_ref):
    za_ref[...] = z_ref[0] + (xa_ref[0] + xb_ref[0])
    mid_ref[...] = own_ref[...] + (xa_ref[1] + xb_ref[1])
    zb_ref[...] = z_ref[1] + (xa_ref[2] + xb_ref[2])


def force_kernel(
    half_depth, own_ref, mid_ref, za_ref, zb_ref, total_ref, velocity_ref, drag_ref, volume_ref,
    force_ref, loads_ref,
):
    place, _, _ = features(own_ref[...], jnp.int32(0), jnp.int32(0), True, half_depth)
    total = total_ref[...]
    pair = (STIFFNESS / PAIR_SCALE) * (place[0:3] * total[4:5] - total[0:3])
    fetched = (mid_ref[...] + (za_ref[...] + zb_ref[...])).astype(F32)
    for k in range(3):
        force = (
            drag_ref[...] * (fetched[k : k + 1] - velocity_ref[k])
            - volume_ref[...] * fetched[3 + k : 4 + k]
            + pair[k : k + 1]
        )
        force_ref[k] = force
        loads_ref[k : k + 1] = force
    loads_ref[3:4] = volume_ref[...]


def side_weights(fraction_row, bins, first, count, rows, low):
    particles = fraction_row.shape[1]
    extent = bins + 2 * MARGIN
    along = fraction_row * (bins * FILTER_SCALE)
    index = lax.broadcasted_iota(jnp.int32, (extent, particles), 0).astype(F32)
    distance = along - (index - (MARGIN - 0.5)) * FILTER_SCALE
    inverse = 1.0 / jnp.sum(jnp.exp2(-(distance * distance)), axis=0, keepdims=True)
    row = lax.broadcasted_iota(jnp.int32, (rows, particles), 0)
    here = row.astype(F32) + first.astype(F32)
    distance = along - (here - (MARGIN - 0.5)) * FILTER_SCALE
    bumps = jnp.exp2(-(distance * distance)) * inverse
    return jnp.where((row >= low) & (row < low + count), bumps, 0.0)


def cross_axis(step, bins):
    return jnp.where(step < 0, bins + MARGIN, 0), jnp.where(step < 0, 0, bins - MARGIN)


def x_part(block, step):
    first, to = cross_axis(step, BX)
    return side_weights(block[0:1], BX, first, MARGIN, 8, 0), to


def y_part(block, step):
    first, _ = cross_axis(step, BY)
    low = jnp.where(step < 0, 0, MARGIN)
    return side_weights(block[1:2], BY, first - low, MARGIN, 8, low), jnp.where(step < 0, 0, BY - 8)


def whole_part(row, bins):
    return side_weights(row, bins, jnp.int32(MARGIN), bins, bins, 0)


def spread_rows(along_x, count_x, along_y, load, spread_ref):
    rows = along_y.shape[0]
    group = max(1, 16 // rows)
    for a in range(0, count_x, group):
        parts = [(along_x[a + i : a + i + 1] * along_y) * load for i in range(group)]
        part = parts[0] if group == 1 else jnp.concatenate(parts, axis=0)
        spread_ref[a * rows : (a + group) * rows] = part.astype(BF16)


def spread_product(along_x, count_x, along_y, load, depth, spread_ref):
    rows = along_y.shape[0]
    spread_rows(along_x, count_x, along_y, load, spread_ref)
    piece = jnp.dot(spread_ref[: count_x * rows], depth, preferred_element_type=F32)
    return piece.reshape(count_x, rows, piece.shape[1])


def filter_own_kernel(scale, own_ref, loads_ref, depth_ref, out_ref, spread_ref):
    own = own_ref[...]
    depth = depth_ref[...]
    along_x = whole_part(own[0:1], BX)
    along_y = whole_part(own[1:2], BY)
    for c in range(4):
        out_ref[c] = spread_product(
            along_x, BX, along_y, loads_ref[c : c + 1] * scale, depth, spread_ref
        )


def filter_x_kernel(scale, xa_ref, xb_ref, la_ref, lb_ref, da_ref, db_ref, out_ref, spread_ref):
    for which, (ref, loads, depth_ref) in enumerate(
        ((xa_ref, la_ref, da_ref), (xb_ref, lb_ref, db_ref))
    ):
        block = ref[1]
        step, _ = partner("gx", which)
        depth = depth_ref[1]
        along_x, _ = x_part(block, step)
        along_y = whole_part(block[1:2], BY)
        for c in range(4):
            out_ref[which, c] = spread_product(
                along_x, MARGIN, along_y, loads[c : c + 1] * scale, depth, spread_ref
            )


def rest_blocks(za_ref, zb_ref, xa_ref, xb_ref):
    for side in range(2):
        for column in range(3):
            if column == 1:
                yield side, column, (za_ref, zb_ref)[side][...]
            else:
                yield side, column, (xa_ref, xb_ref)[column // 2][2 * side]


def filter_rest_kernel(
    scale, za_ref, zb_ref, xa_ref, xb_ref, la_ref, lb_ref, dz_ref, da_ref, db_ref, side_ref,
    field_ref, out_ref, x_ref, y_ref, spread_ref,
):
    c = pl.program_id(0)
    steps = y_steps()
    steps = (steps[0][0], steps[2][0])

    @pl.when(c == 0)
    def _():
        for side, column, block in rest_blocks(za_ref, zb_ref, xa_ref, xb_ref):
            n = 3 * side + column
            y_ref[n] = y_part(block, steps[side])[0]
            if column == 1:
                x_ref[n] = whole_part(block[0:1], BX)
            else:
                x_ref[n, 0:8] = x_part(block, partner("gx", column // 2)[0])[0]

    out_ref[...] = field_ref[...]
    for which in range(2):
        _, to_x = cross_axis(partner("gx", which)[0], BX)
        out_ref[0, pl.ds(to_x, MARGIN)] += side_ref[which, 0]
    for side, loads in enumerate((la_ref, lb_ref)):
        to_y = pl.multiple_of(jnp.where(steps[side] < 0, 0, BY - 8), 8)
        for column in range(3):
            n = 3 * side + column
            if column == 1:
                to_x, count = 0, BX
            else:
                _, to_x = cross_axis(partner("gx", column // 2)[0], BX)
                count = MARGIN
            load = loads[column, pl.ds(c, 1)] * scale
            depth = dz_ref[side] if column == 1 else (da_ref, db_ref)[column // 2][2 * side]
            piece = spread_product(x_ref[n], count, y_ref[n], load, depth, spread_ref)
            out_ref[0, pl.ds(to_x, count), pl.ds(to_y, 8)] += piece


def call(kernel, shapes, args, scratch=(), flops=0, name=None, mib=12, far=()):
    many = isinstance(shapes, list)
    return pl.pallas_call(
        kernel,
        out_shape=shapes,
        in_specs=[
            pl.BlockSpec(memory_space=pltpu.HBM) if i in far else VMEM for i in range(len(args))
        ],
        out_specs=[VMEM] * len(shapes) if many else VMEM,
        scratch_shapes=list(scratch),
        cost_estimate=pl.CostEstimate(flops=flops, bytes_accessed=1 << 16, transcendentals=0),
        compiler_params=pltpu.CompilerParams(vmem_limit_bytes=mib << 20),
        name=name,
    )(*args)


def body(fractions, velocity, drag_rate, volume, owner, element, coords, fluid):
    particles = fractions.shape[3]
    elements = fluid.shape[2]
    depth = 512
    half_depth = 0.5 * depth / BX
    table = fluid.reshape(elements, 6, fluid.shape[4]).transpose(1, 0, 2)
    table = table.reshape(6 * elements, fluid.shape[4])
    basis = jnp.asarray(split_table())
    row = (1, particles)
    planes = (3, 1, particles)
    block = jax.ShapeDtypeStruct((8, particles), F32)
    reply = jax.ShapeDtypeStruct((8, particles), BF16)
    target = pltpu.VMEM((48, particles), BF16)
    weights = pltpu.VMEM((fluid.shape[4], max(particles, 8 * CAP)), BF16)
    cost = particles * particles * 1000

    own = call(
        pack_kernel,
        block,
        (fractions.reshape(planes), owner.reshape(row), element.reshape(row), coords.reshape(planes)),
        flops=1000,
        name="pack",
        mib=60,
    )
    zb = swap(own, "gy", 1)
    za = swap(own, "gy", 0)
    def depths(*lead):
        return jax.ShapeDtypeStruct((*lead, particles, depth), BF16)

    total, values, d_own = call(
        partial(own_kernel, half_depth),
        [block, reply, depths()],
        (own, table, basis),
        (target, weights, pltpu.VMEM(table.shape, BF16), pltpu.VMEM(basis.shape, BF16), pltpu.SemaphoreType.DMA((2,))),
        flops=2 * cost,
        name="own",
        far=(1, 2),
    )
    column = jnp.stack([za, own, zb])
    xb = swap(column, "gx", 1)
    xa = swap(column, "gx", 0)
    total, d_z = call(
        partial(column_kernel, half_depth),
        [block, depths(2)],
        (own, za, zb, total),
        (target,),
        flops=2 * cost,
        name="column",
    )
    reply3 = jax.ShapeDtypeStruct((3, 8, particles), BF16)
    reply2 = jax.ShapeDtypeStruct((2, 8, particles), BF16)
    z_out, xa_out, xb_out = call(
        serve_kernel,
        [reply2, reply3, reply3],
        (za, zb, xa, xb, table, basis),
        (pltpu.VMEM((8, 2 * CAP, particles), BF16), weights),
        flops=2 * cost,
        name="serve",
        mib=12,
    )
    xb_in = swap(xb_out, "gx", 1)
    xa_in = swap(xa_out, "gx", 0)
    total, d_a = call(
        partial(side_kernel, 0, half_depth),
        [block, depths(3)],
        (own, xa, total),
        (target,),
        flops=3 * cost,
        name="side_a",
    )
    mid, za_out, zb_out = call(
        join_kernel, [reply] * 3, (values, z_out, xa_in, xb_in), flops=1000, name="join"
    )
    zb_in = swap(zb_out, "gy", 1)
    za_in = swap(za_out, "gy", 0)
    total, d_b = call(
        partial(side_kernel, 1, half_depth),
        [block, depths(3)],
        (own, xb, total),
        (target,),
        flops=3 * cost,
        name="side_b",
    )
    force, loads = call(
        partial(force_kernel, half_depth),
        [jax.ShapeDtypeStruct(planes, F32), jax.ShapeDtypeStruct((4, particles), F32)],
        (
            own,
            mid,
            za_in,
            zb_in,
            total,
            velocity.reshape(planes),
            drag_rate.reshape(row),
            volume.reshape(row),
        ),
        flops=1000,
        name="force",
    )
    lb = swap(loads, "gx", 1)
    la = swap(loads, "gx", 0)
    scale = BX * BY * depth / particles
    spread = pltpu.VMEM((BX * BY, particles), BF16)
    field = call(
        partial(filter_own_kernel, scale),
        jax.ShapeDtypeStruct((4, BX, BY, depth), F32),
        (own, loads, d_own),
        (spread,),
        flops=2 * cost,
        name="filter_own",
        mib=16,
    )
    load_row = jnp.stack([la, loads, lb])
    lzb = swap(load_row, "gy", 1)
    lza = swap(load_row, "gy", 0)
    sides = call(
        partial(filter_x_kernel, scale),
        jax.ShapeDtypeStruct((2, 4, MARGIN, BY, depth), F32),
        (xa, xb, la, lb, d_a, d_b),
        (spread,),
        flops=2 * cost,
        name="filter_x",
        mib=16,
    )
    field = pl.pallas_call(
        partial(filter_rest_kernel, scale),
        grid=(4,),
        out_shape=jax.ShapeDtypeStruct((4, BX, BY, depth), F32),
        in_specs=[VMEM] * 9
        + [
            pl.BlockSpec((2, 1, MARGIN, BY, depth), lambda c: (0, c, 0, 0, 0)),
            pl.BlockSpec((1, BX, BY, depth), lambda c: (c, 0, 0, 0)),
        ],
        out_specs=pl.BlockSpec((1, BX, BY, depth), lambda c: (c, 0, 0, 0)),
        scratch_shapes=[
            pltpu.VMEM((6, BX, particles), F32),
            pltpu.VMEM((6, 8, particles), F32),
            spread,
        ],
        cost_estimate=pl.CostEstimate(flops=4 * cost, bytes_accessed=1 << 16, transcendentals=0),
        compiler_params=pltpu.CompilerParams(vmem_limit_bytes=16 << 20),
        name="filter_rest",
    )(za, zb, xa, xb, lza, lzb, d_z, d_a, d_b, sides, field)
    return (force.reshape(1, 1, 3, particles), field)


def solution(mesh):
    return jax.shard_map(
        body,
        mesh=mesh,
        in_specs=(
            P("gx", "gy", None, None),
            P("gx", "gy", None, None),
            P("gx", "gy", None),
            P("gx", "gy", None),
            P("gx", "gy", None, None),
            P("gx", "gy", None),
            P("gx", "gy", None, None),
            P("gx", "gy", None, None, None),
        ),
        out_specs=(P("gx", "gy", None, None), P(None, "gx", "gy", None)),
        check_vma=False,
    )
```

time: 145 us -> 56.9 us (0.39)
  other arithmetic: 55.4 us -> 0.02 us
  starting transfers between devices: 49.7 us -> 21.5 us
  Pallas kernels: 0 us -> 27.2 us
  matrix products: 15.2 us -> 0 us
  local copies, waits for them, and re-layouts: 17 us -> 2.42 us
    reduce_sum x15 -> x0, other arithmetic: 36 us -> none  [the longest x4 26 us: one_group(): summed = summed + jnp.sum(offset * closeness[None, :, :], axis=2)]
    ppermute x16 -> x12, starting transfers between devices: 49.7 us -> 21.5 us  [swap(): return lax.ppermute(block, axis, pairs + [(b, a) for a, b in pairs])]
    pallas_call x0 -> x11, Pallas kernels: none -> 27.2 us  [the longest x10 21 us: call(): pl.pallas_call(kernel, out_shape=shapes, in_specs=[pl.BlockSpec(memory_sp...]
    dot_general x18 -> x0, matrix products: 15.2 us -> none  [the longest x9 12.7 us: window_cube(): jnp.einsum('vtn,tl->vnl', scattered_loads, along_depth, preferred_element...]
    mul x30 -> x0, other arithmetic: 10 us -> none  [the longest x12 7.98 us: one_group(): jnp.exp(-jnp.sum(offset * offset, axis=0) / (2.0 * PAIR_WIDTH * PAIR_WIDTH))]
    gather x1 -> x0, local copies, waits for them, and re-layouts: 3.21 us -> none  [body(): flatten_blocks(returned)[:, jnp.minimum(position_index, 9 * CAP - 1)]]
    scatter x1 -> x0, local copies, waits for them, and re-layouts: 3.13 us -> none  [body(): jnp.zeros((4, 9 * CAP + 1), jnp.int32).at[:, position_index].set(payload)]
    another operation x8 -> x2, other arithmetic: 2.7 us -> 0.02 us  [the longest x1 0.01 us: body(): load_row = jnp.stack([la, loads, lb])]
  transfers between devices with their start and end apart: 16 -> 12, of which waited for: 3 -> 4; matrix products, arithmetic and copies ran while one was open for 22% -> 0% of each run, Pallas kernels for 0% -> 31%
where the time goes in v1:
time: 56.9 us; the launch traced here: 56.5 us
  Pallas kernels  27.2 us (48%)
  starting transfers between devices  21.5 us (38%)
  waiting for transfers between devices  4.54 us (8%)
  local copies, waits for them, and re-layouts  2.42 us (4%)
  between operations  0.88 us (2%)
    ppermute x12, starting transfers between devices, swap(): return lax.ppermute(block, axis, pairs + [(b, a) for a, b in pairs])  21.5 us
    pallas_call x10, Pallas kernels, call(): pl.pallas_call(kernel, out_shape=shapes, in_specs=[pl.BlockSpec(memory_sp...  21 us
    pallas_call x1, Pallas kernels, body(): pl.pallas_call(partial(filter_rest_kernel, scale), grid=(4,), out_shape=j...  6.15 us
    ppermute x12, waiting for transfers between devices, swap(): return lax.ppermute(block, axis, pairs + [(b, a) for a, b in pairs])  4.54 us
    unnamed x18, local copies, waits for them, and re-layouts  2.42 us
  transfers between devices with their start and end apart: 12, of which 4 were waited for; matrix products, arithmetic and copies ran while one was open for 0% of the time, Pallas kernels for 31%

profile of v1, /device:TPU:12, one launch (start us, length us, event | category | flops | bytes accessed | tf_op | source)
XLA Modules:
  0.0 56.5 jit_solution(11624877413506649058)
XLA Ops:
  0.6 1.4 %pack.1.own_ref = f32[8,1024]{1,0:T(8,128)} custom-call(f32[3,1,1024]{2,1,0:T(1,128)} %bitcast.32, s32[1,1024]{1,0:T(1,128)} %bitcast.34, s32[1,1024]{1,0:T(1,128)} %bitcast.35, s32[3,1,1024]{2,1,0:T(1,128)} %bitcast.33), custom_call_target="tpu_custom_call" | custom-call | flops 1000 | bytes 65536 | tf_op jit(solution)/shard_map/pack/pallas_call | solution.py:441
  2.0 3.5 %collective-permute-start.1 = (f32[8,1024]{1,0:T(8,128)}, f32[8,1024]{1,0:T(8,128)S(1)}, u32[]{:S(2)}, u32[]{:S(2)}) collective-permute-start(f32[8,1024]{1,0:T(8,128)} %pack.1.own_ref), channel_id=1, source_target_pairs={{1,2},{2,1},{5,6},{6,5},{9,10},{10,9},{13,14},{14,13},{17,18},{18,... | collective-permute-start | bytes 98312 | tf_op jit(solution)/shard_map/ppermute | solution.py:82
  5.5 0.1 collective-permute-start
  5.6 0.0 copy-start
  5.6 0.8 %copy-done = f32[8,1024]{1,0:T(8,128)S(1)} copy-done((f32[8,1024]{1,0:T(8,128)S(1)}, f32[8,1024]{1,0:T(8,128)}, u32[]{:S(2)}) %copy-start) | copy-done | bytes 32792
  6.4 0.0 copy-start.5
  6.4 0.9 %copy-done.5 = bf16[1,1,32,6,512]{4,2,3,1,0:T(8,128)(2,1)S(1)} copy-done((bf16[1,1,32,6,512]{4,2,3,1,0:T(8,128)(2,1)S(1)}, bf16[1,1,32,6,512]{4,2,3,1,0:T(8,128)(2,1)}, u32[]{:S(2)}) %copy-start.5) | copy-done | bytes 196632
  7.3 0.7 %copy-done.7 = bf16[24,64]{1,0:T(8,128)(2,1)S(1)} copy-done((bf16[24,64]{1,0:T(8,128)(2,1)S(1)}, bf16[24,64]{1,0:T(8,128)(2,1)}, u32[]{:S(2)}) %copy-start.7) | copy-done | bytes 3096
  8.0 2.6 %own.1 = (f32[8,1024]{1,0:T(8,128)S(1)}, bf16[8,1024]{1,0:T(8,128)(2,1)S(1)}, bf16[1024,512]{1,0:T(8,128)(2,1)S(1)}) custom-call(f32[8,1024]{1,0:T(8,128)S(1)} %copy-done, bf16[192,512]{1,0:T(8,128)(2,1)S(1)} %bitcast.30, bf16[24,64]{1,0:T(8,128)(2,1)S(1)} %copy-done.7), custom_call_target="tpu_custom_call" | custom-call | flops 2097152000 | bytes 65536 | tf_op jit(solution)/shard_map/own/pallas_call | solution.py:441
  10.6 0.0 collective-permute-done.1.zb_ref.second_ref
  10.6 0.0 collective-permute-done.za_ref.first_ref
  10.6 2.5 %collective-permute-start.3 = (f32[3,8,1024]{2,1,0:T(8,128)S(1)}, f32[3,8,1024]{2,1,0:T(8,128)S(1)}, u32[]{:S(2)}, u32[]{:S(2)}) collective-permute-start(f32[3,8,1024]{2,1,0:T(8,128)S(1)} %pad_maximum_fusion), channel_id=1, source_target_pairs={{4,8},{12,16},{20,24},{8,4},{16,12},{24,20},{5,9},{13,17},{21,25},... | collective-permute-start | bytes 294920 | tf_op jit(solution)/shard_map/ppermute | solution.py:82
  13.1 1.1 %collective-permute-start.2 = (f32[3,8,1024]{2,1,0:T(8,128)S(1)}, f32[3,8,1024]{2,1,0:T(8,128)S(1)}, u32[]{:S(2)}, u32[]{:S(2)}) collective-permute-start(f32[3,8,1024]{2,1,0:T(8,128)S(1)} %pad_maximum_fusion), channel_id=1, source_target_pairs={{0,4},{8,12},{16,20},{24,28},{4,0},{12,8},{20,16},{28,24},{1,5},{9... | collective-permute-start | bytes 294920 | tf_op jit(solution)/shard_map/ppermute | solution.py:82
  14.2 0.0 copy-done.1
  14.2 3.1 %column.1 = (f32[8,1024]{1,0:T(8,128)S(1)}, bf16[2,1024,512]{2,1,0:T(8,128)(2,1)S(1)}) custom-call(f32[8,1024]{1,0:T(8,128)S(1)} %copy-done.1, f32[8,1024]{1,0:T(8,128)S(1)} %collective-permute-done.za_ref.first_ref, f32[8,1024]{1,0:T(8,128)S(1)} %collective-permute-done.1.zb_ref.second_ref, f32[8,1024]{1,0:T(8,128)S(1)} %get-tuple-element.26.sum_ref), custom_call_target="tpu_custom_call" | custom-call | flops 2097152000 | bytes 65536 | tf_op jit(solution)/shard_map/column/pallas_call | solution.py:441
  17.4 0.2 collective-permute-done.3.xb_ref.blocks_ref
  17.6 0.0 collective-permute-done.2.xa_ref.blocks_ref
  17.6 0.0 copy-done.6
  17.6 0.0 copy-done.8
  17.6 1.5 %serve.1 = (bf16[2,8,1024]{2,1,0:T(8,128)(2,1)S(1)}, bf16[3,8,1024]{2,1,0:T(8,128)(2,1)S(1)}, bf16[3,8,1024]{2,1,0:T(8,128)(2,1)S(1)}) custom-call(f32[8,1024]{1,0:T(8,128)S(1)} %collective-permute-done.za_ref.first_ref, f32[8,1024]{1,0:T(8,128)S(1)} %collective-permute-done.1.zb_ref.second_ref, f32[3,8,1024]{2,1,0:T(8,128)S(1)} %collective-permute-done.2.xa_ref.blocks_ref, ...), custom_call_target="tpu_custom_call" | custom-call | flops 2097152000 | bytes 65536 | tf_op jit(solution)/shard_map/serve/pallas_call | solution.py:441
  19.1 0.1 collective-permute-start.4
  19.2 3.2 %collective-permute-start.5 = (bf16[3,8,1024]{2,1,0:T(8,128)(2,1)S(1)}, bf16[3,8,1024]{2,1,0:T(8,128)(2,1)S(1)}, u32[]{:S(2)}, u32[]{:S(2)}) collective-permute-start(bf16[3,8,1024]{2,1,0:T(8,128)(2,1)S(1)} %get-tuple-element.22), channel_id=1, source_target_pairs={{4,8},{12,16},{20,24},{8,4},{16,12},{24,20},{5,9},{13,17},{21,25},... | collective-permute-start | bytes 147464 | tf_op jit(solution)/shard_map/ppermute | solution.py:82
  22.4 4.5 %side_a.1 = (f32[8,1024]{1,0:T(8,128)S(1)}, bf16[3,1024,512]{2,1,0:T(8,128)(2,1)S(1)}) custom-call(f32[8,1024]{1,0:T(8,128)S(1)} %copy-done.1, f32[3,8,1024]{2,1,0:T(8,128)S(1)} %collective-permute-done.2.xa_ref.blocks_ref, f32[8,1024]{1,0:T(8,128)S(1)} %get-tuple-element.27.sum_ref), custom_call_target="tpu_custom_call" | custom-call | flops 3145728000 | bytes 65536 | tf_op jit(solution)/shard_map/side_a/pallas_call | solution.py:441
  26.9 0.0 collective-permute-done.4.xa_ref
  26.9 0.0 collective-permute-done.5.xb_ref
  26.9 2.1 %collective-permute-start.6 = (bf16[8,1024]{1,0:T(8,128)(2,1)S(1)}, bf16[8,1024]{1,0:T(8,128)(2,1)S(1)}, u32[]{:S(2)}, u32[]{:S(2)}) collective-permute-start(bf16[8,1024]{1,0:T(8,128)(2,1)S(1)} %get-tuple-element.24), channel_id=1, source_target_pairs={{0,1},{2,3},{1,0},{3,2},{4,5},{6,7},{5,4},{7,6},{8,9},{10,11},{9,8... | collective-permute-start | bytes 49160 | tf_op jit(solution)/shard_map/ppermute | solution.py:82
  29.0 2.5 %collective-permute-start.7 = (bf16[8,1024]{1,0:T(8,128)(2,1)S(1)}, bf16[8,1024]{1,0:T(8,128)(2,1)S(1)}, u32[]{:S(2)}, u32[]{:S(2)}) collective-permute-start(bf16[8,1024]{1,0:T(8,128)(2,1)S(1)} %get-tuple-element.25), channel_id=1, source_target_pairs={{1,2},{2,1},{5,6},{6,5},{9,10},{10,9},{13,14},{14,13},{17,18},{18,... | collective-permute-start | bytes 49160 | tf_op jit(solution)/shard_map/ppermute | solution.py:82
  31.6 0.0 copy-start.2
  31.6 0.0 copy-start.3
  31.6 0.0 copy-start.4
  31.6 4.5 %side_b.1 = (f32[8,1024]{1,0:T(8,128)S(1)}, bf16[3,1024,512]{2,1,0:T(8,128)(2,1)S(1)}) custom-call(f32[8,1024]{1,0:T(8,128)S(1)} %copy-done.1, f32[3,8,1024]{2,1,0:T(8,128)S(1)} %collective-permute-done.3.xb_ref.blocks_ref, f32[8,1024]{1,0:T(8,128)S(1)} %get-tuple-element.28.sum_ref), custom_call_target="tpu_custom_call" | custom-call | flops 3145728000 | bytes 65536 | tf_op jit(solution)/shard_map/side_b/pallas_call | solution.py:441
  36.1 0.0 collective-permute-done.6.za_ref
  36.1 0.0 collective-permute-done.7.zb_ref
  36.1 0.0 copy-done.2
  36.1 0.0 copy-done.3
  36.1 0.0 copy-done.4
  36.1 0.6 %force.1 = (f32[3,1,1024]{2,1,0:T(1,128)}, f32[4,1024]{1,0:T(4,128)S(1)}) custom-call(f32[8,1024]{1,0:T(8,128)S(1)} %copy-done.1, bf16[8,1024]{1,0:T(8,128)(2,1)S(1)} %get-tuple-element.23.mid_ref, bf16[8,1024]{1,0:T(8,128)(2,1)S(1)} %collective-permute-done.6.za_ref, bf16[8,1024]{1,0:T(8,128)(2,1)S(1)} %collective-permute-done.7.zb_ref, ...), custom_call_target="tpu_custom_call" | custom-call | flops 1000 | bytes 65536 | tf_op jit(solution)/shard_map/force/pallas_call | solution.py:441
  36.8 2.7 %collective-permute-start.9 = (f32[4,1024]{1,0:T(4,128)S(1)}, f32[4,1024]{1,0:T(4,128)S(1)}, u32[]{:S(2)}, u32[]{:S(2)}) collective-permute-start(f32[4,1024]{1,0:T(4,128)S(1)} %get-tuple-element.31.loads_ref), channel_id=1, source_target_pairs={{4,8},{12,16},{20,24},{8,4},{16,12},{24,20},{5,9},{13,17},{21,25},... | collective-permute-start | bytes 49160 | tf_op jit(solution)/shard_map/ppermute | solution.py:82
  39.4 0.2 collective-permute-start.8
  39.6 1.3 %filter_own.1.field_ref = f32[4,16,16,512]{3,2,1,0:T(8,128)S(1)} custom-call(f32[8,1024]{1,0:T(8,128)S(1)} %copy-done.1, f32[4,1024]{1,0:T(4,128)S(1)} %get-tuple-element.31.loads_ref, bf16[1024,512]{1,0:T(8,128)(2,1)S(1)} %get-tuple-element.35.depth_ref), custom_call_target="tpu_custom_call" | custom-call | flops 2097152000 | bytes 65536 | tf_op jit(solution)/shard_map/filter_own/pallas_call | solution.py:441
  40.9 1.8 %collective-permute-done.9.lb_ref = f32[4,1024]{1,0:T(4,128)S(1)} collective-permute-done((f32[4,1024]{1,0:T(4,128)S(1)}, f32[4,1024]{1,0:T(4,128)S(1)}, u32[]{:S(2)}, u32[]{:S(2)}) %collective-permute-start.9) | collective-permute-done | bytes 16416 | tf_op jit(solution)/shard_map/ppermute | solution.py:82
  42.7 0.0 collective-permute-done.8.la_ref
  42.7 3.5 %collective-permute-start.11 = (f32[3,4,1024]{2,1,0:T(4,128)S(1)}, f32[3,4,1024]{2,1,0:T(4,128)S(1)}, u32[]{:S(2)}, u32[]{:S(2)}) collective-permute-start(f32[3,4,1024]{2,1,0:T(4,128)S(1)} %pad_maximum_fusion.1), channel_id=1, source_target_pairs={{1,2},{2,1},{5,6},{6,5},{9,10},{10,9},{13,14},{14,13},{17,18},{18,... | collective-permute-start | bytes 147464 | tf_op jit(solution)/shard_map/ppermute | solution.py:82
  46.2 0.1 collective-permute-start.10
  46.3 1.6 %filter_x.1.side_ref = f32[2,4,4,16,512]{4,3,2,1,0:T(8,128)S(1)} custom-call(f32[3,8,1024]{2,1,0:T(8,128)S(1)} %collective-permute-done.2.xa_ref.blocks_ref, f32[3,8,1024]{2,1,0:T(8,128)S(1)} %collective-permute-done.3.xb_ref.blocks_ref, f32[4,1024]{1,0:T(4,128)S(1)} %collective-permute-done.8.la_ref, f32[4,1024]{1,0:T(4,128)S(1)} %collective-permute-done.9.lb_ref, ...), custom_call_target="tpu_custom_call" | custom-call | flops 2097152000 | bytes 65536 | tf_op jit(solution)/shard_map/filter_x/pallas_call | solution.py:441
  47.9 0.8 %collective-permute-done.11.lb_ref = f32[3,4,1024]{2,1,0:T(4,128)S(1)} collective-permute-done((f32[3,4,1024]{2,1,0:T(4,128)S(1)}, f32[3,4,1024]{2,1,0:T(4,128)S(1)}, u32[]{:S(2)}, u32[]{:S(2)}) %collective-permute-start.11) | collective-permute-done | bytes 49184 | tf_op jit(solution)/shard_map/ppermute | solution.py:82
  48.7 1.7 %collective-permute-done.10.la_ref = f32[3,4,1024]{2,1,0:T(4,128)S(1)} collective-permute-done((f32[3,4,1024]{2,1,0:T(4,128)S(1)}, f32[3,4,1024]{2,1,0:T(4,128)S(1)}, u32[]{:S(2)}, u32[]{:S(2)}) %collective-permute-start.10) | collective-permute-done | bytes 49184 | tf_op jit(solution)/shard_map/ppermute | solution.py:82
  50.4 6.2 %filter_rest.1 = f32[4,16,16,512]{3,2,1,0:T(8,128)} custom-call(f32[8,1024]{1,0:T(8,128)S(1)} %collective-permute-done.za_ref.first_ref, f32[8,1024]{1,0:T(8,128)S(1)} %collective-permute-done.1.zb_ref.second_ref, f32[3,8,1024]{2,1,0:T(8,128)S(1)} %collective-permute-done.2.xa_ref.blocks_ref, f32[3,8,1024]{2,1,0:T(8,128)S(1)} %collective-permute-done.3.xb_ref.blocks_ref, ...), custom_call_target="tpu_custom_call" | custom-call | flops 4194304000 | bytes 65536 | tf_op jit(solution)/shard_map/filter_rest/pallas_call | solution.py:579
  (7 shorter events, 0.0 us)
Async XLA Ops:
  2.0 8.6 %collective-permute-start.1 = (f32[8,1024]{1,0:T(8,128)}, f32[8,1024]{1,0:T(8,128)S(1)}, u32[]{:S(2)}, u32[]{:S(2)}) collective-permute-start(f32[8,1024]{1,0:T(8,128)} %pack.1.own_ref), channel_id=1, source_target_pairs={{1,2},{2,1},{5,6},{6,5},{9,10},{10,9},{13,14},{14,13},{17,18},{18,... | collective-permute-start | bytes 98312 | tf_op jit(solution)/shard_map/ppermute | solution.py:82
  5.5 5.1 %collective-permute-start = (f32[8,1024]{1,0:T(8,128)}, f32[8,1024]{1,0:T(8,128)S(1)}, u32[]{:S(2)}, u32[]{:S(2)}) collective-permute-start(f32[8,1024]{1,0:T(8,128)} %pack.1.own_ref), channel_id=1, source_target_pairs={{0,1},{2,3},{1,0},{3,2},{4,5},{6,7},{5,4},{7,6},{8,9},{10,11},{9,8... | collective-permute-start | bytes 98312 | tf_op jit(solution)/shard_map/ppermute | solution.py:82
  5.6 0.8 %copy-start = (f32[8,1024]{1,0:T(8,128)S(1)}, f32[8,1024]{1,0:T(8,128)}, u32[]{:S(2)}) copy-start(f32[8,1024]{1,0:T(8,128)} %pack.1.own_ref) | copy-start | bytes 98308
  6.4 0.9 %copy-start.5 = (bf16[1,1,32,6,512]{4,2,3,1,0:T(8,128)(2,1)S(1)}, bf16[1,1,32,6,512]{4,2,3,1,0:T(8,128)(2,1)}, u32[]{:S(2)}) copy-start(bf16[1,1,32,6,512]{4,2,3,1,0:T(8,128)(2,1)} %param.16) | copy-start | bytes 589828
  7.3 0.7 %copy-start.7 = (bf16[24,64]{1,0:T(8,128)(2,1)S(1)}, bf16[24,64]{1,0:T(8,128)(2,1)}, u32[]{:S(2)}) copy-start(bf16[24,64]{1,0:T(8,128)(2,1)} %constant.2.clone.far_basis_ref.basis_ref) | copy-start | bytes 9220
  8.0 6.3 %copy-start.1 = (f32[8,1024]{1,0:T(8,128)S(1)}, f32[8,1024]{1,0:T(8,128)}, u32[]{:S(2)}) copy-start(f32[8,1024]{1,0:T(8,128)} %pack.1.own_ref) | copy-start | bytes 98308
  10.6 7.0 %collective-permute-start.3 = (f32[3,8,1024]{2,1,0:T(8,128)S(1)}, f32[3,8,1024]{2,1,0:T(8,128)S(1)}, u32[]{:S(2)}, u32[]{:S(2)}) collective-permute-start(f32[3,8,1024]{2,1,0:T(8,128)S(1)} %pad_maximum_fusion), channel_id=1, source_target_pairs={{4,8},{12,16},{20,24},{8,4},{16,12},{24,20},{5,9},{13,17},{21,25},... | collective-permute-start | bytes 294920 | tf_op jit(solution)/shard_map/ppermute | solution.py:82
  13.1 4.5 %collective-permute-start.2 = (f32[3,8,1024]{2,1,0:T(8,128)S(1)}, f32[3,8,1024]{2,1,0:T(8,128)S(1)}, u32[]{:S(2)}, u32[]{:S(2)}) collective-permute-start(f32[3,8,1024]{2,1,0:T(8,128)S(1)} %pad_maximum_fusion), channel_id=1, source_target_pairs={{0,4},{8,12},{16,20},{24,28},{4,0},{12,8},{20,16},{28,24},{1,5},{9... | collective-permute-start | bytes 294920 | tf_op jit(solution)/shard_map/ppermute | solution.py:82
  14.2 3.4 %copy-start.6 = (bf16[1,1,32,6,512]{4,2,3,1,0:T(8,128)(2,1)S(1)}, bf16[1,1,32,6,512]{4,2,3,1,0:T(8,128)(2,1)}, u32[]{:S(2)}) copy-start(bf16[1,1,32,6,512]{4,2,3,1,0:T(8,128)(2,1)} %param.16) | copy-start | bytes 589828
  14.2 3.4 %copy-start.8 = (bf16[24,64]{1,0:T(8,128)(2,1)S(1)}, bf16[24,64]{1,0:T(8,128)(2,1)}, u32[]{:S(2)}) copy-start(bf16[24,64]{1,0:T(8,128)(2,1)} %constant.2.clone.far_basis_ref.basis_ref) | copy-start | bytes 9220
  19.1 7.8 %collective-permute-start.4 = (bf16[3,8,1024]{2,1,0:T(8,128)(2,1)S(1)}, bf16[3,8,1024]{2,1,0:T(8,128)(2,1)S(1)}, u32[]{:S(2)}, u32[]{:S(2)}) collective-permute-start(bf16[3,8,1024]{2,1,0:T(8,128)(2,1)S(1)} %get-tuple-element.21), channel_id=1, source_target_pairs={{0,4},{8,12},{16,20},{24,28},{4,0},{12,8},{20,16},{28,24},{1,5},{9... | collective-permute-start | bytes 147464 | tf_op jit(solution)/shard_map/ppermute | solution.py:82
  19.2 7.7 %collective-permute-start.5 = (bf16[3,8,1024]{2,1,0:T(8,128)(2,1)S(1)}, bf16[3,8,1024]{2,1,0:T(8,128)(2,1)S(1)}, u32[]{:S(2)}, u32[]{:S(2)}) collective-permute-start(bf16[3,8,1024]{2,1,0:T(8,128)(2,1)S(1)} %get-tuple-element.22), channel_id=1, source_target_pairs={{4,8},{12,16},{20,24},{8,4},{16,12},{24,20},{5,9},{13,17},{21,25},... | collective-permute-start | bytes 147464 | tf_op jit(solution)/shard_map/ppermute | solution.py:82
  26.9 9.1 %collective-permute-start.6 = (bf16[8,1024]{1,0:T(8,128)(2,1)S(1)}, bf16[8,1024]{1,0:T(8,128)(2,1)S(1)}, u32[]{:S(2)}, u32[]{:S(2)}) collective-permute-start(bf16[8,1024]{1,0:T(8,128)(2,1)S(1)} %get-tuple-element.24), channel_id=1, source_target_pairs={{0,1},{2,3},{1,0},{3,2},{4,5},{6,7},{5,4},{7,6},{8,9},{10,11},{9,8... | collective-permute-start | bytes 49160 | tf_op jit(solution)/shard_map/ppermute | solution.py:82
  29.0 7.1 %collective-permute-start.7 = (bf16[8,1024]{1,0:T(8,128)(2,1)S(1)}, bf16[8,1024]{1,0:T(8,128)(2,1)S(1)}, u32[]{:S(2)}, u32[]{:S(2)}) collective-permute-start(bf16[8,1024]{1,0:T(8,128)(2,1)S(1)} %get-tuple-element.25), channel_id=1, source_target_pairs={{1,2},{2,1},{5,6},{6,5},{9,10},{10,9},{13,14},{14,13},{17,18},{18,... | collective-permute-start | bytes 49160 | tf_op jit(solution)/shard_map/ppermute | solution.py:82
  31.6 4.5 %copy-start.2 = (f32[1,1,3,1024]{3,1,2,0:T(1,128)S(1)}, f32[1,1,3,1024]{3,1,2,0:T(1,128)}, u32[]{:S(2)}) copy-start(f32[1,1,3,1024]{3,1,2,0:T(1,128)} %param.10) | copy-start | bytes 36868
  31.6 4.5 %copy-start.3 = (f32[1,1,1024]{2,1,0:T(1,128)S(1)}, f32[1,1,1024]{2,1,0:T(1,128)}, u32[]{:S(2)}) copy-start(f32[1,1,1024]{2,1,0:T(1,128)} %param.11) | copy-start | bytes 12292
  31.6 4.5 %copy-start.4 = (f32[1,1,1024]{2,1,0:T(1,128)S(1)}, f32[1,1,1024]{2,1,0:T(1,128)}, u32[]{:S(2)}) copy-start(f32[1,1,1024]{2,1,0:T(1,128)} %param.12) | copy-start | bytes 12292
  36.8 5.9 %collective-permute-start.9 = (f32[4,1024]{1,0:T(4,128)S(1)}, f32[4,1024]{1,0:T(4,128)S(1)}, u32[]{:S(2)}, u32[]{:S(2)}) collective-permute-start(f32[4,1024]{1,0:T(4,128)S(1)} %get-tuple-element.31.loads_ref), channel_id=1, source_target_pairs={{4,8},{12,16},{20,24},{8,4},{16,12},{24,20},{5,9},{13,17},{21,25},... | collective-permute-start | bytes 49160 | tf_op jit(solution)/shard_map/ppermute | solution.py:82
  39.4 3.3 %collective-permute-start.8 = (f32[4,1024]{1,0:T(4,128)S(1)}, f32[4,1024]{1,0:T(4,128)S(1)}, u32[]{:S(2)}, u32[]{:S(2)}) collective-permute-start(f32[4,1024]{1,0:T(4,128)S(1)} %get-tuple-element.31.loads_ref), channel_id=1, source_target_pairs={{0,4},{8,12},{16,20},{24,28},{4,0},{12,8},{20,16},{28,24},{1,5},{9... | collective-permute-start | bytes 49160 | tf_op jit(solution)/shard_map/ppermute | solution.py:82
  42.7 6.0 %collective-permute-start.11 = (f32[3,4,1024]{2,1,0:T(4,128)S(1)}, f32[3,4,1024]{2,1,0:T(4,128)S(1)}, u32[]{:S(2)}, u32[]{:S(2)}) collective-permute-start(f32[3,4,1024]{2,1,0:T(4,128)S(1)} %pad_maximum_fusion.1), channel_id=1, source_target_pairs={{1,2},{2,1},{5,6},{6,5},{9,10},{10,9},{13,14},{14,13},{17,18},{18,... | collective-permute-start | bytes 147464 | tf_op jit(solution)/shard_map/ppermute | solution.py:82
  46.2 4.2 %collective-permute-start.10 = (f32[3,4,1024]{2,1,0:T(4,128)S(1)}, f32[3,4,1024]{2,1,0:T(4,128)S(1)}, u32[]{:S(2)}, u32[]{:S(2)}) collective-permute-start(f32[3,4,1024]{2,1,0:T(4,128)S(1)} %pad_maximum_fusion.1), channel_id=1, source_target_pairs={{0,1},{2,3},{1,0},{3,2},{4,5},{6,7},{5,4},{7,6},{8,9},{10,11},{9,8... | collective-permute-start | bytes 147464 | tf_op jit(solution)/shard_map/ppermute | solution.py:82

commit v2 on v1

--- a/solution.py
+++ b/solution.py
@@ -125,7 +125,10 @@
     _, source, _ = features(block, step_x, step_y, present, half_depth)
     a, b, c = split3(source)
     rows = jnp.concatenate([a, a, b, b, a, c], axis=0).astype(BF16)
-    values = jnp.concatenate([a, b, c, jnp.zeros_like(a)], axis=0).astype(BF16)
+    row = lax.broadcasted_iota(jnp.int32, a.shape, 0)
+    moved = jnp.where(row < 7, pltpu.roll(b, 4, 0), 0.0)
+    first = jnp.where(row < 3, a, jnp.where(row == 3, 1.0, moved))
+    values = jnp.concatenate([first, jnp.where(row < 3, c, 0.0)], axis=0).astype(BF16)
     width = min(256, particles)
     for start in range(0, particles, width):
         exponent = lax.dot_general(
@@ -140,7 +143,7 @@
         sums = jnp.dot(values, high, preferred_element_type=F32) + jnp.dot(
             values, low, preferred_element_type=F32
         )
-        total_ref[:, start : start + width] += sums[0:8] + sums[8:16] + sums[16:24]
+        total_ref[:, start : start + width] += sums
         depth_ref[start : start + width] = depth_rows(column[start : start + width], depth)
 
 
@@ -181,7 +184,26 @@
     return (lax.axis_index("gx") * lax.axis_size("gy") + lax.axis_index("gy")).astype(F32)
 
 
-def pack_kernel(fractions_ref, owner_ref, element_ref, coords_ref, out_ref):
+def fetch_all(sources, targets, arrived):
+    fetches = [
+        pltpu.make_async_copy(source, target, arrived.at[n])
+        for n, (source, target) in enumerate(zip(sources, targets))
+    ]
+    for fetch in fetches:
+        fetch.start()
+    return fetches
+
+
+def pack_kernel(
+    far_fractions_ref, far_owner_ref, far_element_ref, far_coords_ref, out_ref,
+    fractions_ref, owner_ref, element_ref, coords_ref, arrived,
+):
+    for fetch in fetch_all(
+        (far_fractions_ref, far_owner_ref, far_element_ref, far_coords_ref),
+        (fractions_ref, owner_ref, element_ref, coords_ref),
+        arrived,
+    ):
+        fetch.wait()
     for k in range(3):
         out_ref[k : k + 1] = fractions_ref[k]
         out_ref[5 + k : 6 + k] = coords_ref[k].astype(F32)
@@ -193,12 +215,7 @@
     half_depth, own_ref, far_table_ref, far_basis_ref, total_ref, values_ref, depth_ref,
     target_ref, weight_ref, table_ref, basis_ref, arrived,
 ):
-    fetches = [
-        pltpu.make_async_copy(far_table_ref, table_ref, arrived.at[0]),
-        pltpu.make_async_copy(far_basis_ref, basis_ref, arrived.at[1]),
-    ]
-    for fetch in fetches:
-        fetch.start()
+    fetches = fetch_all((far_table_ref, far_basis_ref), (table_ref, basis_ref), arrived)
     own = own_ref[...]
     _, target = target_rows(own, half_depth)
     target_ref[...] = target
@@ -302,7 +319,8 @@
 ):
     place, _, _ = features(own_ref[...], jnp.int32(0), jnp.int32(0), True, half_depth)
     total = total_ref[...]
-    pair = (STIFFNESS / PAIR_SCALE) * (place[0:3] * total[4:5] - total[0:3])
+    first = total[0:3] + (total[4:7] + total[8:11])
+    pair = (STIFFNESS / PAIR_SCALE) * (place[0:3] * total[3:4] - first)
     fetched = (mid_ref[...] + (za_ref[...] + zb_ref[...])).astype(F32)
     for k in range(3):
         force = (
@@ -375,68 +393,81 @@
         )
 
 
-def filter_x_kernel(scale, xa_ref, xb_ref, la_ref, lb_ref, da_ref, db_ref, out_ref, spread_ref):
+def planes_into(ref, along_x, count_x, along_y):
+    rows = along_y.shape[0]
+    for a in range(count_x):
+        ref[a * rows : (a + 1) * rows] = along_x[a : a + 1] * along_y
+
+
+def scatter_loads(plane, loads, scale, spread_ref):
+    rows = plane.shape[0]
+    count = loads.shape[0]
+    for c in range(count):
+        spread_ref[c * rows : (c + 1) * rows] = (plane * (loads[c : c + 1] * scale)).astype(BF16)
+    return spread_ref[: count * rows]
+
+
+def filter_x_kernel(
+    scale, xa_ref, xb_ref, za_ref, zb_ref, la_ref, lb_ref, da_ref, db_ref,
+    out_ref, mid_ref, corner_ref, plane_ref, spread_ref,
+):
+    depth = out_ref.shape[4]
+    y_offsets = (y_steps()[0][0], y_steps()[2][0])
     for which, (ref, loads, depth_ref) in enumerate(
         ((xa_ref, la_ref, da_ref), (xb_ref, lb_ref, db_ref))
     ):
+        step, _ = partner("gx", which)
         block = ref[1]
-        step, _ = partner("gx", which)
-        depth = depth_ref[1]
-        along_x, _ = x_part(block, step)
-        along_y = whole_part(block[1:2], BY)
-        for c in range(4):
-            out_ref[which, c] = spread_product(
-                along_x, MARGIN, along_y, loads[c : c + 1] * scale, depth, spread_ref
+        planes_into(plane_ref, x_part(block, step)[0], MARGIN, whole_part(block[1:2], BY))
+        spread = scatter_loads(plane_ref[...], loads[...], scale, spread_ref)
+        piece = jnp.dot(spread, depth_ref[1], preferred_element_type=F32)
+        out_ref[which] = piece.reshape(4, MARGIN, BY, depth)
+        for side in range(2):
+            block = ref[2 * side]
+            along_y = y_part(block, y_offsets[side])[0]
+            planes_into(corner_ref.at[2 * side + which], x_part(block, step)[0], MARGIN, along_y)
+    for side, ref in enumerate((za_ref, zb_ref)):
+        block = ref[...]
+        along_y = y_part(block, y_offsets[side])[0]
+        planes_into(mid_ref.at[side], whole_part(block[0:1], BX), BX, along_y)
+
+
+def filter_rest_kernel(
+    scale, mid_ref, corner_ref, la_ref, lb_ref, dz_ref, da_ref, db_ref, side_ref, field_ref,
+    out_ref, sum_ref, spread_ref, sent,
+):
+    depth = out_ref.shape[3]
+    y_offsets = (y_steps()[0][0], y_steps()[2][0])
+    copies = []
+    for side, loads in enumerate((la_ref, lb_ref)):
+        half = pl.ds(pl.multiple_of(jnp.where(y_offsets[side] < 0, 0, BY - 8), 8), 8)
+        sum_ref[side] = field_ref[:, :, half]
+        for which, depth_ref in enumerate((da_ref, db_ref)):
+            to_x = pl.ds(cross_axis(partner("gx", which)[0], BX)[1], MARGIN)
+            plane = corner_ref[2 * side + which]
+            spread = scatter_loads(plane, loads[2 * which], scale, spread_ref)
+            piece = jnp.dot(spread, depth_ref[2 * side], preferred_element_type=F32)
+            sum_ref[side, :, to_x] += (
+                piece.reshape(4, MARGIN, 8, depth) + side_ref[which, :, :, half]
             )
-
-
-def rest_blocks(za_ref, zb_ref, xa_ref, xb_ref):
-    for side in range(2):
-        for column in range(3):
-            if column == 1:
-                yield side, column, (za_ref, zb_ref)[side][...]
-            else:
-                yield side, column, (xa_ref, xb_ref)[column // 2][2 * side]
-
-
-def filter_rest_kernel(
-    scale, za_ref, zb_ref, xa_ref, xb_ref, la_ref, lb_ref, dz_ref, da_ref, db_ref, side_ref,
-    field_ref, out_ref, x_ref, y_ref, spread_ref,
-):
-    c = pl.program_id(0)
-    steps = y_steps()
-    steps = (steps[0][0], steps[2][0])
-
-    @pl.when(c == 0)
-    def _():
-        for side, column, block in rest_blocks(za_ref, zb_ref, xa_ref, xb_ref):
-            n = 3 * side + column
-            y_ref[n] = y_part(block, steps[side])[0]
-            if column == 1:
-                x_ref[n] = whole_part(block[0:1], BX)
-            else:
-                x_ref[n, 0:8] = x_part(block, partner("gx", column // 2)[0])[0]
-
-    out_ref[...] = field_ref[...]
-    for which in range(2):
-        _, to_x = cross_axis(partner("gx", which)[0], BX)
-        out_ref[0, pl.ds(to_x, MARGIN)] += side_ref[which, 0]
-    for side, loads in enumerate((la_ref, lb_ref)):
-        to_y = pl.multiple_of(jnp.where(steps[side] < 0, 0, BY - 8), 8)
-        for column in range(3):
-            n = 3 * side + column
-            if column == 1:
-                to_x, count = 0, BX
-            else:
-                _, to_x = cross_axis(partner("gx", column // 2)[0], BX)
-                count = MARGIN
-            load = loads[column, pl.ds(c, 1)] * scale
-            depth = dz_ref[side] if column == 1 else (da_ref, db_ref)[column // 2][2 * side]
-            piece = spread_product(x_ref[n], count, y_ref[n], load, depth, spread_ref)
-            out_ref[0, pl.ds(to_x, count), pl.ds(to_y, 8)] += piece
-
-
-def call(kernel, shapes, args, scratch=(), flops=0, name=None, mib=12, far=()):
+        for c in range(0, 4, 2):
+            spread = scatter_loads(mid_ref[side], loads[1, c : c + 2], scale, spread_ref)
+            piece = jnp.dot(spread, dz_ref[side], preferred_element_type=F32)
+            sum_ref[side, c : c + 2] += piece.reshape(2, BX, 8, depth)
+            copy = pltpu.make_async_copy(
+                sum_ref.at[side, c : c + 2], out_ref.at[c : c + 2, :, half], sent.at[len(copies)]
+            )
+            copy.start()
+            copies.append(copy)
+    for copy in copies:
+        copy.wait()
+
+
+def far(array):
+    return pltpu.with_memory_space_constraint(array, pltpu.HBM)
+
+
+def call(kernel, shapes, args, scratch=(), flops=0, name=None, mib=12, far=(), far_out=False):
     many = isinstance(shapes, list)
     return pl.pallas_call(
         kernel,
@@ -444,7 +475,11 @@
         in_specs=[
             pl.BlockSpec(memory_space=pltpu.HBM) if i in far else VMEM for i in range(len(args))
         ],
-        out_specs=[VMEM] * len(shapes) if many else VMEM,
+        out_specs=[VMEM] * len(shapes)
+        if many
+        else pl.BlockSpec(memory_space=pltpu.HBM)
+        if far_out
+        else VMEM,
         scratch_shapes=list(scratch),
         cost_estimate=pl.CostEstimate(flops=flops, bytes_accessed=1 << 16, transcendentals=0),
         compiler_params=pltpu.CompilerParams(vmem_limit_bytes=mib << 20),
@@ -464,6 +499,7 @@
     planes = (3, 1, particles)
     block = jax.ShapeDtypeStruct((8, particles), F32)
     reply = jax.ShapeDtypeStruct((8, particles), BF16)
+    sums = jax.ShapeDtypeStruct((16, particles), F32)
     target = pltpu.VMEM((48, particles), BF16)
     weights = pltpu.VMEM((fluid.shape[4], max(particles, 8 * CAP)), BF16)
     cost = particles * particles * 1000
@@ -471,10 +507,26 @@
     own = call(
         pack_kernel,
         block,
-        (fractions.reshape(planes), owner.reshape(row), element.reshape(row), coords.reshape(planes)),
+        tuple(
+            far(x)
+            for x in (
+                fractions.reshape(planes),
+                owner.reshape(row),
+                element.reshape(row),
+                coords.reshape(planes),
+            )
+        ),
+        (
+            pltpu.VMEM(planes, F32),
+            pltpu.VMEM(row, jnp.int32),
+            pltpu.VMEM(row, jnp.int32),
+            pltpu.VMEM(planes, jnp.int32),
+            pltpu.SemaphoreType.DMA((4,)),
+        ),
         flops=1000,
         name="pack",
-        mib=60,
+        mib=4,
+        far=(0, 1, 2, 3),
     )
     zb = swap(own, "gy", 1)
     za = swap(own, "gy", 0)
@@ -483,8 +535,8 @@
 
     total, values, d_own = call(
         partial(own_kernel, half_depth),
-        [block, reply, depths()],
-        (own, table, basis),
+        [sums, reply, depths()],
+        (own, far(table), far(basis)),
         (target, weights, pltpu.VMEM(table.shape, BF16), pltpu.VMEM(basis.shape, BF16), pltpu.SemaphoreType.DMA((2,))),
         flops=2 * cost,
         name="own",
@@ -495,7 +547,7 @@
     xa = swap(column, "gx", 0)
     total, d_z = call(
         partial(column_kernel, half_depth),
-        [block, depths(2)],
+        [sums, depths(2)],
         (own, za, zb, total),
         (target,),
         flops=2 * cost,
@@ -516,7 +568,7 @@
     xa_in = swap(xa_out, "gx", 0)
     total, d_a = call(
         partial(side_kernel, 0, half_depth),
-        [block, depths(3)],
+        [sums, depths(3)],
         (own, xa, total),
         (target,),
         flops=3 * cost,
@@ -529,7 +581,7 @@
     za_in = swap(za_out, "gy", 0)
     total, d_b = call(
         partial(side_kernel, 1, half_depth),
-        [block, depths(3)],
+        [sums, depths(3)],
         (own, xb, total),
         (target,),
         flops=3 * cost,
@@ -567,34 +619,33 @@
     load_row = jnp.stack([la, loads, lb])
     lzb = swap(load_row, "gy", 1)
     lza = swap(load_row, "gy", 0)
-    sides = call(
+    sides, mids, corners = call(
         partial(filter_x_kernel, scale),
-        jax.ShapeDtypeStruct((2, 4, MARGIN, BY, depth), F32),
-        (xa, xb, la, lb, d_a, d_b),
-        (spread,),
+        [
+            jax.ShapeDtypeStruct((2, 4, MARGIN, BY, depth), F32),
+            jax.ShapeDtypeStruct((2, BX * 8, particles), F32),
+            jax.ShapeDtypeStruct((4, MARGIN * 8, particles), F32),
+        ],
+        (xa, xb, za, zb, la, lb, d_a, d_b),
+        (pltpu.VMEM((MARGIN * BY, particles), F32), spread),
         flops=2 * cost,
         name="filter_x",
         mib=16,
     )
-    field = pl.pallas_call(
+    field = call(
         partial(filter_rest_kernel, scale),
-        grid=(4,),
-        out_shape=jax.ShapeDtypeStruct((4, BX, BY, depth), F32),
-        in_specs=[VMEM] * 9
-        + [
-            pl.BlockSpec((2, 1, MARGIN, BY, depth), lambda c: (0, c, 0, 0, 0)),
-            pl.BlockSpec((1, BX, BY, depth), lambda c: (c, 0, 0, 0)),
-        ],
-        out_specs=pl.BlockSpec((1, BX, BY, depth), lambda c: (c, 0, 0, 0)),
-        scratch_shapes=[
-            pltpu.VMEM((6, BX, particles), F32),
-            pltpu.VMEM((6, 8, particles), F32),
+        jax.ShapeDtypeStruct((4, BX, BY, depth), F32),
+        (mids, corners, lza, lzb, d_z, d_a, d_b, sides, field),
+        (
+            pltpu.VMEM((2, 4, BX, 8, depth), F32),
             spread,
-        ],
-        cost_estimate=pl.CostEstimate(flops=4 * cost, bytes_accessed=1 << 16, transcendentals=0),
-        compiler_params=pltpu.CompilerParams(vmem_limit_bytes=16 << 20),
+            pltpu.SemaphoreType.DMA((4,)),
+        ),
+        flops=4 * cost,
         name="filter_rest",
-    )(za, zb, xa, xb, lza, lzb, d_z, d_a, d_b, sides, field)
+        mib=16,
+        far_out=True,
+    )
     return (force.reshape(1, 1, 3, particles), field)
 
 

time: 56.9 us -> 50.4 us (0.89)
  Pallas kernels: 27.2 us -> 22.6 us
  local copies, waits for them, and re-layouts: 2.42 us -> 0.03 us
  waiting for transfers between devices: 4.54 us -> 6.43 us
  starting transfers between devices: 21.5 us -> 20 us
    pallas_call x1 -> x0, Pallas kernels: 6.15 us -> none  [body(): pl.pallas_call(partial(filter_rest_kernel, scale), grid=(4,), out_shape=j...]
    unnamed x18 -> x10, local copies, waits for them, and re-layouts: 2.42 us -> 0.03 us
    ppermute x12, waiting for transfers between devices: 4.54 us -> 6.43 us  [swap(): return lax.ppermute(block, axis, pairs + [(b, a) for a, b in pairs])]
    pallas_call x10 -> x11, Pallas kernels: 21 us -> 22.6 us  [call(): pl.pallas_call(kernel, out_shape=shapes, in_specs=[pl.BlockSpec(memory_sp...]
    ppermute x12, starting transfers between devices: 21.5 us -> 20 us  [swap(): return lax.ppermute(block, axis, pairs + [(b, a) for a, b in pairs])]
  transfers between devices with their start and end apart: 12 -> 12, of which waited for: 4 -> 5; matrix products, arithmetic and copies ran while one was open for 0% -> 0% of each run, Pallas kernels for 31% -> 34%
where the time goes in v2:
time: 50.4 us; the launch traced here: 50 us
  Pallas kernels  22.6 us (45%)
  starting transfers between devices  20 us (40%)
  waiting for transfers between devices  6.43 us (13%)
  between operations  1 us (2%)
    pallas_call x11, Pallas kernels, call(): pl.pallas_call(kernel, out_shape=shapes, in_specs=[pl.BlockSpec(memory_sp...  22.6 us
    ppermute x12, starting transfers between devices, swap(): return lax.ppermute(block, axis, pairs + [(b, a) for a, b in pairs])  20 us
    ppermute x12, waiting for transfers between devices, swap(): return lax.ppermute(block, axis, pairs + [(b, a) for a, b in pairs])  6.43 us
  transfers between devices with their start and end apart: 12, of which 5 were waited for; matrix products, arithmetic and copies ran while one was open for 0% of the time, Pallas kernels for 34%

profile of v2, /device:TPU:12, one launch (start us, length us, event | category | flops | bytes accessed | tf_op | source)
XLA Modules:
  0.0 50.0 jit_solution(1970869075809385611)
XLA Ops:
  0.6 0.8 %pack.1.own_ref = f32[8,1024]{1,0:T(8,128)S(1)} custom-call(f32[3,1,1024]{2,1,0:T(1,128)} %bitcast.32, s32[1,1024]{1,0:T(1,128)} %bitcast.34, s32[1,1024]{1,0:T(1,128)} %bitcast.35, s32[3,1,1024]{2,1,0:T(1,128)} %bitcast.33), custom_call_target="tpu_custom_call" | custom-call | flops 1000 | bytes 65536 | tf_op jit(solution)/shard_map/pack/pallas_call | solution.py:472
  1.4 3.5 %collective-permute-start.1 = (f32[8,1024]{1,0:T(8,128)S(1)}, f32[8,1024]{1,0:T(8,128)S(1)}, u32[]{:S(2)}, u32[]{:S(2)}) collective-permute-start(f32[8,1024]{1,0:T(8,128)S(1)} %pack.1.own_ref), channel_id=1, source_target_pairs={{1,2},{2,1},{5,6},{6,5},{9,10},{10,9},{13,14},{14,13},{17,18},{18,... | collective-permute-start | bytes 98312 | tf_op jit(solution)/shard_map/ppermute | solution.py:82
  4.9 0.1 collective-permute-start
  5.0 2.4 %own.1 = (f32[16,1024]{1,0:T(8,128)S(1)}, bf16[8,1024]{1,0:T(8,128)(2,1)S(1)}, bf16[1024,512]{1,0:T(8,128)(2,1)S(1)}) custom-call(f32[8,1024]{1,0:T(8,128)S(1)} %pack.1.own_ref, bf16[192,512]{1,0:T(8,128)(2,1)} %bitcast.30, bf16[24,64]{1,0:T(8,128)(2,1)} %constant.2.clone.far_basis_ref.basis_ref), custom_call_target="tpu_custom_call" | custom-call | flops 2097152000 | bytes 65536 | tf_op jit(solution)/shard_map/own/pallas_call | solution.py:472
  7.4 0.0 collective-permute-done.1.zb_ref.second_ref
  7.4 1.5 %collective-permute-done.za_ref.first_ref = f32[8,1024]{1,0:T(8,128)S(1)} collective-permute-done((f32[8,1024]{1,0:T(8,128)S(1)}, f32[8,1024]{1,0:T(8,128)S(1)}, u32[]{:S(2)}, u32[]{:S(2)}) %collective-permute-start) | collective-permute-done | bytes 32800 | tf_op jit(solution)/shard_map/ppermute | solution.py:82
  8.9 1.9 %collective-permute-start.3 = (f32[3,8,1024]{2,1,0:T(8,128)S(1)}, f32[3,8,1024]{2,1,0:T(8,128)S(1)}, u32[]{:S(2)}, u32[]{:S(2)}) collective-permute-start(f32[3,8,1024]{2,1,0:T(8,128)S(1)} %pad_maximum_fusion), channel_id=1, source_target_pairs={{4,8},{12,16},{20,24},{8,4},{16,12},{24,20},{5,9},{13,17},{21,25},... | collective-permute-start | bytes 294920 | tf_op jit(solution)/shard_map/ppermute | solution.py:82
  10.8 1.7 %collective-permute-start.2 = (f32[3,8,1024]{2,1,0:T(8,128)S(1)}, f32[3,8,1024]{2,1,0:T(8,128)S(1)}, u32[]{:S(2)}, u32[]{:S(2)}) collective-permute-start(f32[3,8,1024]{2,1,0:T(8,128)S(1)} %pad_maximum_fusion), channel_id=1, source_target_pairs={{0,4},{8,12},{16,20},{24,28},{4,0},{12,8},{20,16},{28,24},{1,5},{9... | collective-permute-start | bytes 294920 | tf_op jit(solution)/shard_map/ppermute | solution.py:82
  12.5 0.0 copy-start.3
  12.5 0.0 copy-start.4
  12.5 3.1 %column.1 = (f32[16,1024]{1,0:T(8,128)S(1)}, bf16[2,1024,512]{2,1,0:T(8,128)(2,1)S(1)}) custom-call(f32[8,1024]{1,0:T(8,128)S(1)} %pack.1.own_ref, f32[8,1024]{1,0:T(8,128)S(1)} %collective-permute-done.za_ref.first_ref, f32[8,1024]{1,0:T(8,128)S(1)} %collective-permute-done.1.zb_ref.second_ref, f32[16,1024]{1,0:T(8,128)S(1)} %get-tuple-element.29.sum_ref), custom_call_target="tpu_custom_call" | custom-call | flops 2097152000 | bytes 65536 | tf_op jit(solution)/shard_map/column/pallas_call | solution.py:472
  15.6 0.3 collective-permute-done.3.xb_ref.blocks_ref
  15.9 0.0 collective-permute-done.2.xa_ref.blocks_ref
  15.9 0.0 copy-done.3
  15.9 0.0 copy-done.4
  15.9 1.5 %serve.1 = (bf16[2,8,1024]{2,1,0:T(8,128)(2,1)S(1)}, bf16[3,8,1024]{2,1,0:T(8,128)(2,1)S(1)}, bf16[3,8,1024]{2,1,0:T(8,128)(2,1)S(1)}) custom-call(f32[8,1024]{1,0:T(8,128)S(1)} %collective-permute-done.za_ref.first_ref, f32[8,1024]{1,0:T(8,128)S(1)} %collective-permute-done.1.zb_ref.second_ref, f32[3,8,1024]{2,1,0:T(8,128)S(1)} %collective-permute-done.2.xa_ref.blocks_ref, ...), custom_call_target="tpu_custom_call" | custom-call | flops 2097152000 | bytes 65536 | tf_op jit(solution)/shard_map/serve/pallas_call | solution.py:472
  17.4 0.1 collective-permute-start.4
  17.5 3.2 %collective-permute-start.5 = (bf16[3,8,1024]{2,1,0:T(8,128)(2,1)S(1)}, bf16[3,8,1024]{2,1,0:T(8,128)(2,1)S(1)}, u32[]{:S(2)}, u32[]{:S(2)}) collective-permute-start(bf16[3,8,1024]{2,1,0:T(8,128)(2,1)S(1)} %get-tuple-element.25), channel_id=1, source_target_pairs={{4,8},{12,16},{20,24},{8,4},{16,12},{24,20},{5,9},{13,17},{21,25},... | collective-permute-start | bytes 147464 | tf_op jit(solution)/shard_map/ppermute | solution.py:82
  20.7 4.5 %side_a.1 = (f32[16,1024]{1,0:T(8,128)S(1)}, bf16[3,1024,512]{2,1,0:T(8,128)(2,1)S(1)}) custom-call(f32[8,1024]{1,0:T(8,128)S(1)} %pack.1.own_ref, f32[3,8,1024]{2,1,0:T(8,128)S(1)} %collective-permute-done.2.xa_ref.blocks_ref, f32[16,1024]{1,0:T(8,128)S(1)} %get-tuple-element.30.sum_ref), custom_call_target="tpu_custom_call" | custom-call | flops 3145728000 | bytes 65536 | tf_op jit(solution)/shard_map/side_a/pallas_call | solution.py:472
  25.2 0.0 collective-permute-done.4.xa_ref
  25.2 0.0 collective-permute-done.5.xb_ref
  25.2 0.6 %collective-permute-start.6 = (bf16[8,1024]{1,0:T(8,128)(2,1)S(1)}, bf16[8,1024]{1,0:T(8,128)(2,1)S(1)}, u32[]{:S(2)}, u32[]{:S(2)}) collective-permute-start(bf16[8,1024]{1,0:T(8,128)(2,1)S(1)} %get-tuple-element.27), channel_id=1, source_target_pairs={{0,1},{2,3},{1,0},{3,2},{4,5},{6,7},{5,4},{7,6},{8,9},{10,11},{9,8... | collective-permute-start | bytes 49160 | tf_op jit(solution)/shard_map/ppermute | solution.py:82
  25.8 2.5 %collective-permute-start.7 = (bf16[8,1024]{1,0:T(8,128)(2,1)S(1)}, bf16[8,1024]{1,0:T(8,128)(2,1)S(1)}, u32[]{:S(2)}, u32[]{:S(2)}) collective-permute-start(bf16[8,1024]{1,0:T(8,128)(2,1)S(1)} %get-tuple-element.28), channel_id=1, source_target_pairs={{1,2},{2,1},{5,6},{6,5},{9,10},{10,9},{13,14},{14,13},{17,18},{18,... | collective-permute-start | bytes 49160 | tf_op jit(solution)/shard_map/ppermute | solution.py:82
  28.3 0.0 copy-start
  28.3 0.0 copy-start.1
  28.3 0.0 copy-start.2
  28.4 4.5 %side_b.1 = (f32[16,1024]{1,0:T(8,128)S(1)}, bf16[3,1024,512]{2,1,0:T(8,128)(2,1)S(1)}) custom-call(f32[8,1024]{1,0:T(8,128)S(1)} %pack.1.own_ref, f32[3,8,1024]{2,1,0:T(8,128)S(1)} %collective-permute-done.3.xb_ref.blocks_ref, f32[16,1024]{1,0:T(8,128)S(1)} %get-tuple-element.31.sum_ref), custom_call_target="tpu_custom_call" | custom-call | flops 3145728000 | bytes 65536 | tf_op jit(solution)/shard_map/side_b/pallas_call | solution.py:472
  32.9 0.0 collective-permute-done.6.za_ref
  32.9 0.0 collective-permute-done.7.zb_ref
  32.9 0.0 copy-done
  32.9 0.0 copy-done.1
  32.9 0.0 copy-done.2
  32.9 0.6 %force.1 = (f32[3,1,1024]{2,1,0:T(1,128)}, f32[4,1024]{1,0:T(4,128)S(1)}) custom-call(f32[8,1024]{1,0:T(8,128)S(1)} %pack.1.own_ref, bf16[8,1024]{1,0:T(8,128)(2,1)S(1)} %get-tuple-element.26.mid_ref, bf16[8,1024]{1,0:T(8,128)(2,1)S(1)} %collective-permute-done.6.za_ref, bf16[8,1024]{1,0:T(8,128)(2,1)S(1)} %collective-permute-done.7.zb_ref, ...), custom_call_target="tpu_custom_call" | custom-call | flops 1000 | bytes 65536 | tf_op jit(solution)/shard_map/force/pallas_call | solution.py:472
  33.5 2.7 %collective-permute-start.9 = (f32[4,1024]{1,0:T(4,128)S(1)}, f32[4,1024]{1,0:T(4,128)S(1)}, u32[]{:S(2)}, u32[]{:S(2)}) collective-permute-start(f32[4,1024]{1,0:T(4,128)S(1)} %get-tuple-element.34.loads_ref), channel_id=1, source_target_pairs={{4,8},{12,16},{20,24},{8,4},{16,12},{24,20},{5,9},{13,17},{21,25},... | collective-permute-start | bytes 49160 | tf_op jit(solution)/shard_map/ppermute | solution.py:82
  36.2 0.2 collective-permute-start.8
  36.5 1.3 %filter_own.1.field_ref = f32[4,16,16,512]{3,2,1,0:T(8,128)S(1)} custom-call(f32[8,1024]{1,0:T(8,128)S(1)} %pack.1.own_ref, f32[4,1024]{1,0:T(4,128)S(1)} %get-tuple-element.34.loads_ref, bf16[1024,512]{1,0:T(8,128)(2,1)S(1)} %get-tuple-element.41.depth_ref), custom_call_target="tpu_custom_call" | custom-call | flops 2097152000 | bytes 65536 | tf_op jit(solution)/shard_map/filter_own/pallas_call | solution.py:472
  37.7 1.8 %collective-permute-done.9.lb_ref = f32[4,1024]{1,0:T(4,128)S(1)} collective-permute-done((f32[4,1024]{1,0:T(4,128)S(1)}, f32[4,1024]{1,0:T(4,128)S(1)}, u32[]{:S(2)}, u32[]{:S(2)}) %collective-permute-start.9) | collective-permute-done | bytes 16416 | tf_op jit(solution)/shard_map/ppermute | solution.py:82
  39.5 0.0 collective-permute-done.8.la_ref
  39.5 3.5 %collective-permute-start.11 = (f32[3,4,1024]{2,1,0:T(4,128)S(1)}, f32[3,4,1024]{2,1,0:T(4,128)S(1)}, u32[]{:S(2)}, u32[]{:S(2)}) collective-permute-start(f32[3,4,1024]{2,1,0:T(4,128)S(1)} %pad_maximum_fusion.1), channel_id=1, source_target_pairs={{1,2},{2,1},{5,6},{6,5},{9,10},{10,9},{13,14},{14,13},{17,18},{18,... | collective-permute-start | bytes 147464 | tf_op jit(solution)/shard_map/ppermute | solution.py:82
  43.0 0.1 collective-permute-start.10
  43.1 1.2 %filter_x.1 = (f32[2,4,4,16,512]{4,3,2,1,0:T(8,128)S(1)}, f32[2,128,1024]{2,1,0:T(8,128)S(1)}, f32[4,32,1024]{2,1,0:T(8,128)S(1)}) custom-call(f32[3,8,1024]{2,1,0:T(8,128)S(1)} %collective-permute-done.2.xa_ref.blocks_ref, f32[3,8,1024]{2,1,0:T(8,128)S(1)} %collective-permute-done.3.xb_ref.blocks_ref, f32[8,1024]{1,0:T(8,128)S(1)} %collective-permute-done.za_ref.first_ref, ...), custom_call_target="tpu_custom_call" | custom-call | flops 2097152000 | bytes 65536 | tf_op jit(solution)/shard_map/filter_x/pallas_call | solution.py:472
  44.3 1.2 %collective-permute-done.11.lb_ref = f32[3,4,1024]{2,1,0:T(4,128)S(1)} collective-permute-done((f32[3,4,1024]{2,1,0:T(4,128)S(1)}, f32[3,4,1024]{2,1,0:T(4,128)S(1)}, u32[]{:S(2)}, u32[]{:S(2)}) %collective-permute-start.11) | collective-permute-done | bytes 49184 | tf_op jit(solution)/shard_map/ppermute | solution.py:82
  45.5 1.7 %collective-permute-done.10.la_ref = f32[3,4,1024]{2,1,0:T(4,128)S(1)} collective-permute-done((f32[3,4,1024]{2,1,0:T(4,128)S(1)}, f32[3,4,1024]{2,1,0:T(4,128)S(1)}, u32[]{:S(2)}, u32[]{:S(2)}) %collective-permute-start.10) | collective-permute-done | bytes 49184 | tf_op jit(solution)/shard_map/ppermute | solution.py:82
  47.2 2.7 %filter_rest.1 = f32[4,16,16,512]{3,2,1,0:T(8,128)} custom-call(f32[2,128,1024]{2,1,0:T(8,128)S(1)} %get-tuple-element.37.mid_ref, f32[4,32,1024]{2,1,0:T(8,128)S(1)} %get-tuple-element.38.corner_ref, f32[3,4,1024]{2,1,0:T(4,128)S(1)} %collective-permute-done.10.la_ref, f32[3,4,1024]{2,1,0:T(4,128)S(1)} %collective-permute-done.11.lb_ref, ...), custom_call_target="tpu_custom_call" | custom-call | flops 4194304000 | bytes 65536 | tf_op jit(solution)/shard_map/filter_rest/pallas_call | solution.py:472
  (3 shorter events, 0.0 us)
Async XLA Ops:
  1.4 6.0 %collective-permute-start.1 = (f32[8,1024]{1,0:T(8,128)S(1)}, f32[8,1024]{1,0:T(8,128)S(1)}, u32[]{:S(2)}, u32[]{:S(2)}) collective-permute-start(f32[8,1024]{1,0:T(8,128)S(1)} %pack.1.own_ref), channel_id=1, source_target_pairs={{1,2},{2,1},{5,6},{6,5},{9,10},{10,9},{13,14},{14,13},{17,18},{18,... | collective-permute-start | bytes 98312 | tf_op jit(solution)/shard_map/ppermute | solution.py:82
  4.9 4.0 %collective-permute-start = (f32[8,1024]{1,0:T(8,128)S(1)}, f32[8,1024]{1,0:T(8,128)S(1)}, u32[]{:S(2)}, u32[]{:S(2)}) collective-permute-start(f32[8,1024]{1,0:T(8,128)S(1)} %pack.1.own_ref), channel_id=1, source_target_pairs={{0,1},{2,3},{1,0},{3,2},{4,5},{6,7},{5,4},{7,6},{8,9},{10,11},{9,8... | collective-permute-start | bytes 98312 | tf_op jit(solution)/shard_map/ppermute | solution.py:82
  8.9 7.0 %collective-permute-start.3 = (f32[3,8,1024]{2,1,0:T(8,128)S(1)}, f32[3,8,1024]{2,1,0:T(8,128)S(1)}, u32[]{:S(2)}, u32[]{:S(2)}) collective-permute-start(f32[3,8,1024]{2,1,0:T(8,128)S(1)} %pad_maximum_fusion), channel_id=1, source_target_pairs={{4,8},{12,16},{20,24},{8,4},{16,12},{24,20},{5,9},{13,17},{21,25},... | collective-permute-start | bytes 294920 | tf_op jit(solution)/shard_map/ppermute | solution.py:82
  10.8 5.1 %collective-permute-start.2 = (f32[3,8,1024]{2,1,0:T(8,128)S(1)}, f32[3,8,1024]{2,1,0:T(8,128)S(1)}, u32[]{:S(2)}, u32[]{:S(2)}) collective-permute-start(f32[3,8,1024]{2,1,0:T(8,128)S(1)} %pad_maximum_fusion), channel_id=1, source_target_pairs={{0,4},{8,12},{16,20},{24,28},{4,0},{12,8},{20,16},{28,24},{1,5},{9... | collective-permute-start | bytes 294920 | tf_op jit(solution)/shard_map/ppermute | solution.py:82
  12.5 3.4 %copy-start.3 = (bf16[1,1,32,6,512]{4,2,3,1,0:T(8,128)(2,1)S(1)}, bf16[1,1,32,6,512]{4,2,3,1,0:T(8,128)(2,1)}, u32[]{:S(2)}) copy-start(bf16[1,1,32,6,512]{4,2,3,1,0:T(8,128)(2,1)} %param.16) | copy-start | bytes 589828
  12.5 3.4 %copy-start.4 = (bf16[24,64]{1,0:T(8,128)(2,1)S(1)}, bf16[24,64]{1,0:T(8,128)(2,1)}, u32[]{:S(2)}) copy-start(bf16[24,64]{1,0:T(8,128)(2,1)} %constant.2.clone.far_basis_ref.basis_ref) | copy-start | bytes 9220
  17.4 7.8 %collective-permute-start.4 = (bf16[3,8,1024]{2,1,0:T(8,128)(2,1)S(1)}, bf16[3,8,1024]{2,1,0:T(8,128)(2,1)S(1)}, u32[]{:S(2)}, u32[]{:S(2)}) collective-permute-start(bf16[3,8,1024]{2,1,0:T(8,128)(2,1)S(1)} %get-tuple-element.24), channel_id=1, source_target_pairs={{0,4},{8,12},{16,20},{24,28},{4,0},{12,8},{20,16},{28,24},{1,5},{9... | collective-permute-start | bytes 147464 | tf_op jit(solution)/shard_map/ppermute | solution.py:82
  17.5 7.7 %collective-permute-start.5 = (bf16[3,8,1024]{2,1,0:T(8,128)(2,1)S(1)}, bf16[3,8,1024]{2,1,0:T(8,128)(2,1)S(1)}, u32[]{:S(2)}, u32[]{:S(2)}) collective-permute-start(bf16[3,8,1024]{2,1,0:T(8,128)(2,1)S(1)} %get-tuple-element.25), channel_id=1, source_target_pairs={{4,8},{12,16},{20,24},{8,4},{16,12},{24,20},{5,9},{13,17},{21,25},... | collective-permute-start | bytes 147464 | tf_op jit(solution)/shard_map/ppermute | solution.py:82
  25.2 7.6 %collective-permute-start.6 = (bf16[8,1024]{1,0:T(8,128)(2,1)S(1)}, bf16[8,1024]{1,0:T(8,128)(2,1)S(1)}, u32[]{:S(2)}, u32[]{:S(2)}) collective-permute-start(bf16[8,1024]{1,0:T(8,128)(2,1)S(1)} %get-tuple-element.27), channel_id=1, source_target_pairs={{0,1},{2,3},{1,0},{3,2},{4,5},{6,7},{5,4},{7,6},{8,9},{10,11},{9,8... | collective-permute-start | bytes 49160 | tf_op jit(solution)/shard_map/ppermute | solution.py:82
  25.8 7.1 %collective-permute-start.7 = (bf16[8,1024]{1,0:T(8,128)(2,1)S(1)}, bf16[8,1024]{1,0:T(8,128)(2,1)S(1)}, u32[]{:S(2)}, u32[]{:S(2)}) collective-permute-start(bf16[8,1024]{1,0:T(8,128)(2,1)S(1)} %get-tuple-element.28), channel_id=1, source_target_pairs={{1,2},{2,1},{5,6},{6,5},{9,10},{10,9},{13,14},{14,13},{17,18},{18,... | collective-permute-start | bytes 49160 | tf_op jit(solution)/shard_map/ppermute | solution.py:82
  28.3 4.6 %copy-start = (f32[1,1,3,1024]{3,1,2,0:T(1,128)S(1)}, f32[1,1,3,1024]{3,1,2,0:T(1,128)}, u32[]{:S(2)}) copy-start(f32[1,1,3,1024]{3,1,2,0:T(1,128)} %param.10) | copy-start | bytes 36868
  28.3 4.6 %copy-start.1 = (f32[1,1,1024]{2,1,0:T(1,128)S(1)}, f32[1,1,1024]{2,1,0:T(1,128)}, u32[]{:S(2)}) copy-start(f32[1,1,1024]{2,1,0:T(1,128)} %param.11) | copy-start | bytes 12292
  28.3 4.5 %copy-start.2 = (f32[1,1,1024]{2,1,0:T(1,128)S(1)}, f32[1,1,1024]{2,1,0:T(1,128)}, u32[]{:S(2)}) copy-start(f32[1,1,1024]{2,1,0:T(1,128)} %param.12) | copy-start | bytes 12292
  33.5 5.9 %collective-permute-start.9 = (f32[4,1024]{1,0:T(4,128)S(1)}, f32[4,1024]{1,0:T(4,128)S(1)}, u32[]{:S(2)}, u32[]{:S(2)}) collective-permute-start(f32[4,1024]{1,0:T(4,128)S(1)} %get-tuple-element.34.loads_ref), channel_id=1, source_target_pairs={{4,8},{12,16},{20,24},{8,4},{16,12},{24,20},{5,9},{13,17},{21,25},... | collective-permute-start | bytes 49160 | tf_op jit(solution)/shard_map/ppermute | solution.py:82
  36.2 3.2 %collective-permute-start.8 = (f32[4,1024]{1,0:T(4,128)S(1)}, f32[4,1024]{1,0:T(4,128)S(1)}, u32[]{:S(2)}, u32[]{:S(2)}) collective-permute-start(f32[4,1024]{1,0:T(4,128)S(1)} %get-tuple-element.34.loads_ref), channel_id=1, source_target_pairs={{0,4},{8,12},{16,20},{24,28},{4,0},{12,8},{20,16},{28,24},{1,5},{9... | collective-permute-start | bytes 49160 | tf_op jit(solution)/shard_map/ppermute | solution.py:82
  39.5 6.0 %collective-permute-start.11 = (f32[3,4,1024]{2,1,0:T(4,128)S(1)}, f32[3,4,1024]{2,1,0:T(4,128)S(1)}, u32[]{:S(2)}, u32[]{:S(2)}) collective-permute-start(f32[3,4,1024]{2,1,0:T(4,128)S(1)} %pad_maximum_fusion.1), channel_id=1, source_target_pairs={{1,2},{2,1},{5,6},{6,5},{9,10},{10,9},{13,14},{14,13},{17,18},{18,... | collective-permute-start | bytes 147464 | tf_op jit(solution)/shard_map/ppermute | solution.py:82
  43.0 4.2 %collective-permute-start.10 = (f32[3,4,1024]{2,1,0:T(4,128)S(1)}, f32[3,4,1024]{2,1,0:T(4,128)S(1)}, u32[]{:S(2)}, u32[]{:S(2)}) collective-permute-start(f32[3,4,1024]{2,1,0:T(4,128)S(1)} %pad_maximum_fusion.1), channel_id=1, source_target_pairs={{0,1},{2,3},{1,0},{3,2},{4,5},{6,7},{5,4},{7,6},{8,9},{10,11},{9,8... | collective-permute-start | bytes 147464 | tf_op jit(solution)/shard_map/ppermute | solution.py:82

commit v3 on v2

--- a/solution.py
+++ b/solution.py
@@ -8,6 +8,7 @@
 from jax.experimental import pallas as pl
 from jax.experimental.pallas import tpu as pltpu
 from jax.sharding import PartitionSpec as P
+
 
 BX = 16
 BY = 16
@@ -467,7 +468,7 @@
     return pltpu.with_memory_space_constraint(array, pltpu.HBM)
 
 
-def call(kernel, shapes, args, scratch=(), flops=0, name=None, mib=12, far=(), far_out=False):
+def call(kernel, shapes, args, scratch=(), flops=0, mib=12, far=(), far_out=False):
     many = isinstance(shapes, list)
     return pl.pallas_call(
         kernel,
@@ -483,11 +484,10 @@
         scratch_shapes=list(scratch),
         cost_estimate=pl.CostEstimate(flops=flops, bytes_accessed=1 << 16, transcendentals=0),
         compiler_params=pltpu.CompilerParams(vmem_limit_bytes=mib << 20),
-        name=name,
     )(*args)
 
 
-def body(fractions, velocity, drag_rate, volume, owner, element, coords, fluid):
+def step(fractions, velocity, drag_rate, volume, owner, element, coords, fluid):
     particles = fractions.shape[3]
     elements = fluid.shape[2]
     depth = 512
@@ -524,7 +524,6 @@
             pltpu.SemaphoreType.DMA((4,)),
         ),
         flops=1000,
-        name="pack",
         mib=4,
         far=(0, 1, 2, 3),
     )
@@ -539,7 +538,6 @@
         (own, far(table), far(basis)),
         (target, weights, pltpu.VMEM(table.shape, BF16), pltpu.VMEM(basis.shape, BF16), pltpu.SemaphoreType.DMA((2,))),
         flops=2 * cost,
-        name="own",
         far=(1, 2),
     )
     column = jnp.stack([za, own, zb])
@@ -551,7 +549,6 @@
         (own, za, zb, total),
         (target,),
         flops=2 * cost,
-        name="column",
     )
     reply3 = jax.ShapeDtypeStruct((3, 8, particles), BF16)
     reply2 = jax.ShapeDtypeStruct((2, 8, particles), BF16)
@@ -561,7 +558,6 @@
         (za, zb, xa, xb, table, basis),
         (pltpu.VMEM((8, 2 * CAP, particles), BF16), weights),
         flops=2 * cost,
-        name="serve",
         mib=12,
     )
     xb_in = swap(xb_out, "gx", 1)
@@ -572,11 +568,8 @@
         (own, xa, total),
         (target,),
         flops=3 * cost,
-        name="side_a",
-    )
-    mid, za_out, zb_out = call(
-        join_kernel, [reply] * 3, (values, z_out, xa_in, xb_in), flops=1000, name="join"
-    )
+    )
+    mid, za_out, zb_out = call(join_kernel, [reply] * 3, (values, z_out, xa_in, xb_in), flops=1000)
     zb_in = swap(zb_out, "gy", 1)
     za_in = swap(za_out, "gy", 0)
     total, d_b = call(
@@ -585,7 +578,6 @@
         (own, xb, total),
         (target,),
         flops=3 * cost,
-        name="side_b",
     )
     force, loads = call(
         partial(force_kernel, half_depth),
@@ -601,7 +593,6 @@
             volume.reshape(row),
         ),
         flops=1000,
-        name="force",
     )
     lb = swap(loads, "gx", 1)
     la = swap(loads, "gx", 0)
@@ -613,7 +604,6 @@
         (own, loads, d_own),
         (spread,),
         flops=2 * cost,
-        name="filter_own",
         mib=16,
     )
     load_row = jnp.stack([la, loads, lb])
@@ -629,7 +619,6 @@
         (xa, xb, za, zb, la, lb, d_a, d_b),
         (pltpu.VMEM((MARGIN * BY, particles), F32), spread),
         flops=2 * cost,
-        name="filter_x",
         mib=16,
     )
     field = call(
@@ -642,7 +631,6 @@
             pltpu.SemaphoreType.DMA((4,)),
         ),
         flops=4 * cost,
-        name="filter_rest",
         mib=16,
         far_out=True,
     )
@@ -651,7 +639,7 @@
 
 def solution(mesh):
     return jax.shard_map(
-        body,
+        step,
         mesh=mesh,
         in_specs=(
             P("gx", "gy", None, None),

time: 50.4 us -> 50.4 us (level)
  no operation moved by 1% of the time
where the time goes in v3:
time: 50.4 us; the launch traced here: 50 us
  Pallas kernels  22.6 us (45%)
  starting transfers between devices  20 us (40%)
  waiting for transfers between devices  6.43 us (13%)
  between operations  1 us (2%)
    pallas_call x11, Pallas kernels, call(): pl.pallas_call(kernel, out_shape=shapes, in_specs=[pl.BlockSpec(memory_sp...  22.6 us
    ppermute x12, starting transfers between devices, swap(): return lax.ppermute(block, axis, pairs + [(b, a) for a, b in pairs])  20 us
    ppermute x12, waiting for transfers between devices, swap(): return lax.ppermute(block, axis, pairs + [(b, a) for a, b in pairs])  6.43 us
  transfers between devices with their start and end apart: 12, of which 5 were waited for; matrix products, arithmetic and copies ran while one was open for 0% of the time, Pallas kernels for 34%

profile of v3, /device:TPU:12, one launch (start us, length us, event | category | flops | bytes accessed | tf_op | source)
XLA Modules:
  0.0 50.0 jit_solution(1970869075809385611)
XLA Ops:
  0.6 0.8 %shard_map.104.own_ref = f32[8,1024]{1,0:T(8,128)S(1)} custom-call(f32[3,1,1024]{2,1,0:T(1,128)} %bitcast.32, s32[1,1024]{1,0:T(1,128)} %bitcast.34, s32[1,1024]{1,0:T(1,128)} %bitcast.35, s32[3,1,1024]{2,1,0:T(1,128)} %bitcast.33), custom_call_target="tpu_custom_call" | custom-call | flops 1000 | bytes 65536 | tf_op jit(solution)/shard_map/pallas_call | solution.py:473
  1.4 3.5 %collective-permute-start.1 = (f32[8,1024]{1,0:T(8,128)S(1)}, f32[8,1024]{1,0:T(8,128)S(1)}, u32[]{:S(2)}, u32[]{:S(2)}) collective-permute-start(f32[8,1024]{1,0:T(8,128)S(1)} %shard_map.104.own_ref), channel_id=1, source_target_pairs={{1,2},{2,1},{5,6},{6,5},{9,10},{10,9},{13,14},{14,13},{17,18},{18,... | collective-permute-start | bytes 98312 | tf_op jit(solution)/shard_map/ppermute | solution.py:83
  4.9 0.1 collective-permute-start
  5.0 2.4 %shard_map.105 = (f32[16,1024]{1,0:T(8,128)S(1)}, bf16[8,1024]{1,0:T(8,128)(2,1)S(1)}, bf16[1024,512]{1,0:T(8,128)(2,1)S(1)}) custom-call(f32[8,1024]{1,0:T(8,128)S(1)} %shard_map.104.own_ref, bf16[192,512]{1,0:T(8,128)(2,1)} %bitcast.30, bf16[24,64]{1,0:T(8,128)(2,1)} %constant.2.clone.far_basis_ref.basis_ref), custom_call_target="tpu_custom_call" | custom-call | flops 2097152000 | bytes 65536 | tf_op jit(solution)/shard_map/pallas_call | solution.py:473
  7.4 0.0 collective-permute-done.1.zb_ref.second_ref
  7.4 1.5 %collective-permute-done.za_ref.first_ref = f32[8,1024]{1,0:T(8,128)S(1)} collective-permute-done((f32[8,1024]{1,0:T(8,128)S(1)}, f32[8,1024]{1,0:T(8,128)S(1)}, u32[]{:S(2)}, u32[]{:S(2)}) %collective-permute-start) | collective-permute-done | bytes 32800 | tf_op jit(solution)/shard_map/ppermute | solution.py:83
  8.9 1.9 %collective-permute-start.3 = (f32[3,8,1024]{2,1,0:T(8,128)S(1)}, f32[3,8,1024]{2,1,0:T(8,128)S(1)}, u32[]{:S(2)}, u32[]{:S(2)}) collective-permute-start(f32[3,8,1024]{2,1,0:T(8,128)S(1)} %pad_maximum_fusion), channel_id=1, source_target_pairs={{4,8},{12,16},{20,24},{8,4},{16,12},{24,20},{5,9},{13,17},{21,25},... | collective-permute-start | bytes 294920 | tf_op jit(solution)/shard_map/ppermute | solution.py:83
  10.8 1.7 %collective-permute-start.2 = (f32[3,8,1024]{2,1,0:T(8,128)S(1)}, f32[3,8,1024]{2,1,0:T(8,128)S(1)}, u32[]{:S(2)}, u32[]{:S(2)}) collective-permute-start(f32[3,8,1024]{2,1,0:T(8,128)S(1)} %pad_maximum_fusion), channel_id=1, source_target_pairs={{0,4},{8,12},{16,20},{24,28},{4,0},{12,8},{20,16},{28,24},{1,5},{9... | collective-permute-start | bytes 294920 | tf_op jit(solution)/shard_map/ppermute | solution.py:83
  12.5 0.0 copy-start.3
  12.5 0.0 copy-start.4
  12.5 3.1 %shard_map.108 = (f32[16,1024]{1,0:T(8,128)S(1)}, bf16[2,1024,512]{2,1,0:T(8,128)(2,1)S(1)}) custom-call(f32[8,1024]{1,0:T(8,128)S(1)} %shard_map.104.own_ref, f32[8,1024]{1,0:T(8,128)S(1)} %collective-permute-done.za_ref.first_ref, f32[8,1024]{1,0:T(8,128)S(1)} %collective-permute-done.1.zb_ref.second_ref, f32[16,1024]{1,0:T(8,128)S(1)} %get-tuple-element.29.sum_ref), custom_call_target="tpu_custom_call" | custom-call | flops 2097152000 | bytes 65536 | tf_op jit(solution)/shard_map/pallas_call | solution.py:473
  15.6 0.3 collective-permute-done.3.xb_ref.blocks_ref
  15.9 0.0 collective-permute-done.2.xa_ref.blocks_ref
  15.9 0.0 copy-done.3
  15.9 0.0 copy-done.4
  15.9 1.5 %shard_map.106 = (bf16[2,8,1024]{2,1,0:T(8,128)(2,1)S(1)}, bf16[3,8,1024]{2,1,0:T(8,128)(2,1)S(1)}, bf16[3,8,1024]{2,1,0:T(8,128)(2,1)S(1)}) custom-call(f32[8,1024]{1,0:T(8,128)S(1)} %collective-permute-done.za_ref.first_ref, f32[8,1024]{1,0:T(8,128)S(1)} %collective-permute-done.1.zb_ref.second_ref, ...), custom_call_target="tpu_custom_call" | custom-call | flops 2097152000 | bytes 65536 | tf_op jit(solution)/shard_map/pallas_call | solution.py:473
  17.4 0.1 collective-permute-start.4
  17.5 3.2 %collective-permute-start.5 = (bf16[3,8,1024]{2,1,0:T(8,128)(2,1)S(1)}, bf16[3,8,1024]{2,1,0:T(8,128)(2,1)S(1)}, u32[]{:S(2)}, u32[]{:S(2)}) collective-permute-start(bf16[3,8,1024]{2,1,0:T(8,128)(2,1)S(1)} %get-tuple-element.25), channel_id=1, source_target_pairs={{4,8},{12,16},{20,24},{8,4},{16,12},{24,20},{5,9},{13,17},{21,25},... | collective-permute-start | bytes 147464 | tf_op jit(solution)/shard_map/ppermute | solution.py:83
  20.7 4.5 %shard_map.109 = (f32[16,1024]{1,0:T(8,128)S(1)}, bf16[3,1024,512]{2,1,0:T(8,128)(2,1)S(1)}) custom-call(f32[8,1024]{1,0:T(8,128)S(1)} %shard_map.104.own_ref, f32[3,8,1024]{2,1,0:T(8,128)S(1)} %collective-permute-done.2.xa_ref.blocks_ref, f32[16,1024]{1,0:T(8,128)S(1)} %get-tuple-element.30.sum_ref), custom_call_target="tpu_custom_call" | custom-call | flops 3145728000 | bytes 65536 | tf_op jit(solution)/shard_map/pallas_call | solution.py:473
  25.2 0.0 collective-permute-done.4.xa_ref
  25.2 0.0 collective-permute-done.5.xb_ref
  25.2 0.6 %collective-permute-start.6 = (bf16[8,1024]{1,0:T(8,128)(2,1)S(1)}, bf16[8,1024]{1,0:T(8,128)(2,1)S(1)}, u32[]{:S(2)}, u32[]{:S(2)}) collective-permute-start(bf16[8,1024]{1,0:T(8,128)(2,1)S(1)} %get-tuple-element.27), channel_id=1, source_target_pairs={{0,1},{2,3},{1,0},{3,2},{4,5},{6,7},{5,4},{7,6},{8,9},{10,11},{9,8... | collective-permute-start | bytes 49160 | tf_op jit(solution)/shard_map/ppermute | solution.py:83
  25.8 2.5 %collective-permute-start.7 = (bf16[8,1024]{1,0:T(8,128)(2,1)S(1)}, bf16[8,1024]{1,0:T(8,128)(2,1)S(1)}, u32[]{:S(2)}, u32[]{:S(2)}) collective-permute-start(bf16[8,1024]{1,0:T(8,128)(2,1)S(1)} %get-tuple-element.28), channel_id=1, source_target_pairs={{1,2},{2,1},{5,6},{6,5},{9,10},{10,9},{13,14},{14,13},{17,18},{18,... | collective-permute-start | bytes 49160 | tf_op jit(solution)/shard_map/ppermute | solution.py:83
  28.3 0.0 copy-start
  28.3 0.0 copy-start.1
  28.3 0.0 copy-start.2
  28.4 4.5 %shard_map.110 = (f32[16,1024]{1,0:T(8,128)S(1)}, bf16[3,1024,512]{2,1,0:T(8,128)(2,1)S(1)}) custom-call(f32[8,1024]{1,0:T(8,128)S(1)} %shard_map.104.own_ref, f32[3,8,1024]{2,1,0:T(8,128)S(1)} %collective-permute-done.3.xb_ref.blocks_ref, f32[16,1024]{1,0:T(8,128)S(1)} %get-tuple-element.31.sum_ref), custom_call_target="tpu_custom_call" | custom-call | flops 3145728000 | bytes 65536 | tf_op jit(solution)/shard_map/pallas_call | solution.py:473
  32.9 0.0 collective-permute-done.6.za_ref
  32.9 0.0 collective-permute-done.7.zb_ref
  32.9 0.0 copy-done
  32.9 0.0 copy-done.1
  32.9 0.0 copy-done.2
  32.9 0.6 %shard_map.111 = (f32[3,1,1024]{2,1,0:T(1,128)}, f32[4,1024]{1,0:T(4,128)S(1)}) custom-call(f32[8,1024]{1,0:T(8,128)S(1)} %shard_map.104.own_ref, bf16[8,1024]{1,0:T(8,128)(2,1)S(1)} %get-tuple-element.26.mid_ref, bf16[8,1024]{1,0:T(8,128)(2,1)S(1)} %collective-permute-done.6.za_ref, bf16[8,1024]{1,0:T(8,128)(2,1)S(1)} %collective-permute-done.7.zb_ref, ...), custom_call_target="tpu_custom_call" | custom-call | flops 1000 | bytes 65536 | tf_op jit(solution)/shard_map/pallas_call | solution.py:473
  33.5 2.7 %collective-permute-start.9 = (f32[4,1024]{1,0:T(4,128)S(1)}, f32[4,1024]{1,0:T(4,128)S(1)}, u32[]{:S(2)}, u32[]{:S(2)}) collective-permute-start(f32[4,1024]{1,0:T(4,128)S(1)} %get-tuple-element.34.loads_ref), channel_id=1, source_target_pairs={{4,8},{12,16},{20,24},{8,4},{16,12},{24,20},{5,9},{13,17},{21,25},... | collective-permute-start | bytes 49160 | tf_op jit(solution)/shard_map/ppermute | solution.py:83
  36.2 0.2 collective-permute-start.8
  36.5 1.3 %shard_map.113.field_ref = f32[4,16,16,512]{3,2,1,0:T(8,128)S(1)} custom-call(f32[8,1024]{1,0:T(8,128)S(1)} %shard_map.104.own_ref, f32[4,1024]{1,0:T(4,128)S(1)} %get-tuple-element.34.loads_ref, bf16[1024,512]{1,0:T(8,128)(2,1)S(1)} %get-tuple-element.41.depth_ref), custom_call_target="tpu_custom_call" | custom-call | flops 2097152000 | bytes 65536 | tf_op jit(solution)/shard_map/pallas_call | solution.py:473
  37.7 1.8 %collective-permute-done.9.lb_ref = f32[4,1024]{1,0:T(4,128)S(1)} collective-permute-done((f32[4,1024]{1,0:T(4,128)S(1)}, f32[4,1024]{1,0:T(4,128)S(1)}, u32[]{:S(2)}, u32[]{:S(2)}) %collective-permute-start.9) | collective-permute-done | bytes 16416 | tf_op jit(solution)/shard_map/ppermute | solution.py:83
  39.5 0.0 collective-permute-done.8.la_ref
  39.5 3.5 %collective-permute-start.11 = (f32[3,4,1024]{2,1,0:T(4,128)S(1)}, f32[3,4,1024]{2,1,0:T(4,128)S(1)}, u32[]{:S(2)}, u32[]{:S(2)}) collective-permute-start(f32[3,4,1024]{2,1,0:T(4,128)S(1)} %pad_maximum_fusion.1), channel_id=1, source_target_pairs={{1,2},{2,1},{5,6},{6,5},{9,10},{10,9},{13,14},{14,13},{17,18},{18,... | collective-permute-start | bytes 147464 | tf_op jit(solution)/shard_map/ppermute | solution.py:83
  43.0 0.1 collective-permute-start.10
  43.1 1.2 %shard_map.112 = (f32[2,4,4,16,512]{4,3,2,1,0:T(8,128)S(1)}, f32[2,128,1024]{2,1,0:T(8,128)S(1)}, f32[4,32,1024]{2,1,0:T(8,128)S(1)}) custom-call(f32[3,8,1024]{2,1,0:T(8,128)S(1)} %collective-permute-done.2.xa_ref.blocks_ref, f32[3,8,1024]{2,1,0:T(8,128)S(1)} %collective-permute-done.3.xb_ref.blocks_ref, ...), custom_call_target="tpu_custom_call" | custom-call | flops 2097152000 | bytes 65536 | tf_op jit(solution)/shard_map/pallas_call | solution.py:473
  44.3 1.2 %collective-permute-done.11.lb_ref = f32[3,4,1024]{2,1,0:T(4,128)S(1)} collective-permute-done((f32[3,4,1024]{2,1,0:T(4,128)S(1)}, f32[3,4,1024]{2,1,0:T(4,128)S(1)}, u32[]{:S(2)}, u32[]{:S(2)}) %collective-permute-start.11) | collective-permute-done | bytes 49184 | tf_op jit(solution)/shard_map/ppermute | solution.py:83
  45.5 1.7 %collective-permute-done.10.la_ref = f32[3,4,1024]{2,1,0:T(4,128)S(1)} collective-permute-done((f32[3,4,1024]{2,1,0:T(4,128)S(1)}, f32[3,4,1024]{2,1,0:T(4,128)S(1)}, u32[]{:S(2)}, u32[]{:S(2)}) %collective-permute-start.10) | collective-permute-done | bytes 49184 | tf_op jit(solution)/shard_map/ppermute | solution.py:83
  47.2 2.7 %shard_map.114 = f32[4,16,16,512]{3,2,1,0:T(8,128)} custom-call(f32[2,128,1024]{2,1,0:T(8,128)S(1)} %get-tuple-element.37.mid_ref, f32[4,32,1024]{2,1,0:T(8,128)S(1)} %get-tuple-element.38.corner_ref, f32[3,4,1024]{2,1,0:T(4,128)S(1)} %collective-permute-done.10.la_ref, f32[3,4,1024]{2,1,0:T(4,128)S(1)} %collective-permute-done.11.lb_ref, ...), custom_call_target="tpu_custom_call" | custom-call | flops 4194304000 | bytes 65536 | tf_op jit(solution)/shard_map/pallas_call | solution.py:473
  (3 shorter events, 0.0 us)
Async XLA Ops:
  1.4 6.0 %collective-permute-start.1 = (f32[8,1024]{1,0:T(8,128)S(1)}, f32[8,1024]{1,0:T(8,128)S(1)}, u32[]{:S(2)}, u32[]{:S(2)}) collective-permute-start(f32[8,1024]{1,0:T(8,128)S(1)} %shard_map.104.own_ref), channel_id=1, source_target_pairs={{1,2},{2,1},{5,6},{6,5},{9,10},{10,9},{13,14},{14,13},{17,18},{18,... | collective-permute-start | bytes 98312 | tf_op jit(solution)/shard_map/ppermute | solution.py:83
  4.9 4.0 %collective-permute-start = (f32[8,1024]{1,0:T(8,128)S(1)}, f32[8,1024]{1,0:T(8,128)S(1)}, u32[]{:S(2)}, u32[]{:S(2)}) collective-permute-start(f32[8,1024]{1,0:T(8,128)S(1)} %shard_map.104.own_ref), channel_id=1, source_target_pairs={{0,1},{2,3},{1,0},{3,2},{4,5},{6,7},{5,4},{7,6},{8,9},{10,11},{9,8... | collective-permute-start | bytes 98312 | tf_op jit(solution)/shard_map/ppermute | solution.py:83
  8.9 7.0 %collective-permute-start.3 = (f32[3,8,1024]{2,1,0:T(8,128)S(1)}, f32[3,8,1024]{2,1,0:T(8,128)S(1)}, u32[]{:S(2)}, u32[]{:S(2)}) collective-permute-start(f32[3,8,1024]{2,1,0:T(8,128)S(1)} %pad_maximum_fusion), channel_id=1, source_target_pairs={{4,8},{12,16},{20,24},{8,4},{16,12},{24,20},{5,9},{13,17},{21,25},... | collective-permute-start | bytes 294920 | tf_op jit(solution)/shard_map/ppermute | solution.py:83
  10.8 5.1 %collective-permute-start.2 = (f32[3,8,1024]{2,1,0:T(8,128)S(1)}, f32[3,8,1024]{2,1,0:T(8,128)S(1)}, u32[]{:S(2)}, u32[]{:S(2)}) collective-permute-start(f32[3,8,1024]{2,1,0:T(8,128)S(1)} %pad_maximum_fusion), channel_id=1, source_target_pairs={{0,4},{8,12},{16,20},{24,28},{4,0},{12,8},{20,16},{28,24},{1,5},{9... | collective-permute-start | bytes 294920 | tf_op jit(solution)/shard_map/ppermute | solution.py:83
  12.5 3.4 %copy-start.3 = (bf16[1,1,32,6,512]{4,2,3,1,0:T(8,128)(2,1)S(1)}, bf16[1,1,32,6,512]{4,2,3,1,0:T(8,128)(2,1)}, u32[]{:S(2)}) copy-start(bf16[1,1,32,6,512]{4,2,3,1,0:T(8,128)(2,1)} %param.16) | copy-start | bytes 589828
  12.5 3.4 %copy-start.4 = (bf16[24,64]{1,0:T(8,128)(2,1)S(1)}, bf16[24,64]{1,0:T(8,128)(2,1)}, u32[]{:S(2)}) copy-start(bf16[24,64]{1,0:T(8,128)(2,1)} %constant.2.clone.far_basis_ref.basis_ref) | copy-start | bytes 9220
  17.4 7.8 %collective-permute-start.4 = (bf16[3,8,1024]{2,1,0:T(8,128)(2,1)S(1)}, bf16[3,8,1024]{2,1,0:T(8,128)(2,1)S(1)}, u32[]{:S(2)}, u32[]{:S(2)}) collective-permute-start(bf16[3,8,1024]{2,1,0:T(8,128)(2,1)S(1)} %get-tuple-element.24), channel_id=1, source_target_pairs={{0,4},{8,12},{16,20},{24,28},{4,0},{12,8},{20,16},{28,24},{1,5},{9... | collective-permute-start | bytes 147464 | tf_op jit(solution)/shard_map/ppermute | solution.py:83
  17.5 7.7 %collective-permute-start.5 = (bf16[3,8,1024]{2,1,0:T(8,128)(2,1)S(1)}, bf16[3,8,1024]{2,1,0:T(8,128)(2,1)S(1)}, u32[]{:S(2)}, u32[]{:S(2)}) collective-permute-start(bf16[3,8,1024]{2,1,0:T(8,128)(2,1)S(1)} %get-tuple-element.25), channel_id=1, source_target_pairs={{4,8},{12,16},{20,24},{8,4},{16,12},{24,20},{5,9},{13,17},{21,25},... | collective-permute-start | bytes 147464 | tf_op jit(solution)/shard_map/ppermute | solution.py:83
  25.2 7.6 %collective-permute-start.6 = (bf16[8,1024]{1,0:T(8,128)(2,1)S(1)}, bf16[8,1024]{1,0:T(8,128)(2,1)S(1)}, u32[]{:S(2)}, u32[]{:S(2)}) collective-permute-start(bf16[8,1024]{1,0:T(8,128)(2,1)S(1)} %get-tuple-element.27), channel_id=1, source_target_pairs={{0,1},{2,3},{1,0},{3,2},{4,5},{6,7},{5,4},{7,6},{8,9},{10,11},{9,8... | collective-permute-start | bytes 49160 | tf_op jit(solution)/shard_map/ppermute | solution.py:83
  25.8 7.1 %collective-permute-start.7 = (bf16[8,1024]{1,0:T(8,128)(2,1)S(1)}, bf16[8,1024]{1,0:T(8,128)(2,1)S(1)}, u32[]{:S(2)}, u32[]{:S(2)}) collective-permute-start(bf16[8,1024]{1,0:T(8,128)(2,1)S(1)} %get-tuple-element.28), channel_id=1, source_target_pairs={{1,2},{2,1},{5,6},{6,5},{9,10},{10,9},{13,14},{14,13},{17,18},{18,... | collective-permute-start | bytes 49160 | tf_op jit(solution)/shard_map/ppermute | solution.py:83
  28.3 4.6 %copy-start = (f32[1,1,3,1024]{3,1,2,0:T(1,128)S(1)}, f32[1,1,3,1024]{3,1,2,0:T(1,128)}, u32[]{:S(2)}) copy-start(f32[1,1,3,1024]{3,1,2,0:T(1,128)} %param.10) | copy-start | bytes 36868
  28.3 4.6 %copy-start.1 = (f32[1,1,1024]{2,1,0:T(1,128)S(1)}, f32[1,1,1024]{2,1,0:T(1,128)}, u32[]{:S(2)}) copy-start(f32[1,1,1024]{2,1,0:T(1,128)} %param.11) | copy-start | bytes 12292
  28.3 4.5 %copy-start.2 = (f32[1,1,1024]{2,1,0:T(1,128)S(1)}, f32[1,1,1024]{2,1,0:T(1,128)}, u32[]{:S(2)}) copy-start(f32[1,1,1024]{2,1,0:T(1,128)} %param.12) | copy-start | bytes 12292
  33.5 5.9 %collective-permute-start.9 = (f32[4,1024]{1,0:T(4,128)S(1)}, f32[4,1024]{1,0:T(4,128)S(1)}, u32[]{:S(2)}, u32[]{:S(2)}) collective-permute-start(f32[4,1024]{1,0:T(4,128)S(1)} %get-tuple-element.34.loads_ref), channel_id=1, source_target_pairs={{4,8},{12,16},{20,24},{8,4},{16,12},{24,20},{5,9},{13,17},{21,25},... | collective-permute-start | bytes 49160 | tf_op jit(solution)/shard_map/ppermute | solution.py:83
  36.2 3.2 %collective-permute-start.8 = (f32[4,1024]{1,0:T(4,128)S(1)}, f32[4,1024]{1,0:T(4,128)S(1)}, u32[]{:S(2)}, u32[]{:S(2)}) collective-permute-start(f32[4,1024]{1,0:T(4,128)S(1)} %get-tuple-element.34.loads_ref), channel_id=1, source_target_pairs={{0,4},{8,12},{16,20},{24,28},{4,0},{12,8},{20,16},{28,24},{1,5},{9... | collective-permute-start | bytes 49160 | tf_op jit(solution)/shard_map/ppermute | solution.py:83
  39.5 6.0 %collective-permute-start.11 = (f32[3,4,1024]{2,1,0:T(4,128)S(1)}, f32[3,4,1024]{2,1,0:T(4,128)S(1)}, u32[]{:S(2)}, u32[]{:S(2)}) collective-permute-start(f32[3,4,1024]{2,1,0:T(4,128)S(1)} %pad_maximum_fusion.1), channel_id=1, source_target_pairs={{1,2},{2,1},{5,6},{6,5},{9,10},{10,9},{13,14},{14,13},{17,18},{18,... | collective-permute-start | bytes 147464 | tf_op jit(solution)/shard_map/ppermute | solution.py:83
  43.0 4.2 %collective-permute-start.10 = (f32[3,4,1024]{2,1,0:T(4,128)S(1)}, f32[3,4,1024]{2,1,0:T(4,128)S(1)}, u32[]{:S(2)}, u32[]{:S(2)}) collective-permute-start(f32[3,4,1024]{2,1,0:T(4,128)S(1)} %pad_maximum_fusion.1), channel_id=1, source_target_pairs={{0,1},{2,3},{1,0},{3,2},{4,5},{6,7},{5,4},{7,6},{8,9},{10,11},{9,8... | collective-permute-start | bytes 147464 | tf_op jit(solution)/shard_map/ppermute | solution.py:83
